TPU v7x, 256 devices: a whole 4x4x8 slice. The times are simulated.
256 devices in a mesh: seq: 32 (over z, x_hi, core), fsdp: 8 (over y, x_lo).
Axes of the slice: x: 4 (x_hi: 2, x_lo: 2; x = x_hi * 2 + x_lo), y: 4, z: 8, core: 2. Of those that a mesh axis runs over, the one named last changes fastest.
Arguments:
- queries: bfloat16 [8, 4096, 2048], P('fsdp', 'seq'), may hold values from -6 to 6
- key_vectors: bfloat16 [8, 4096, 2048], P('fsdp', 'seq'), may hold values from -6 to 6
- value_vectors: bfloat16 [8, 4096, 2048], P('fsdp', 'seq'), may hold values from -6 to 6
- out_grad: bfloat16 [8, 4096, 2048], P('fsdp', 'seq'), may hold values from -6 to 6
- out_weight: bfloat16 [2048, 2048], P(None, 'fsdp'), may hold values from -0.125 to 0.125
Outputs:
- query_grad: bfloat16 [8, 4096, 2048], P('fsdp', 'seq')
- key_grad: bfloat16 [8, 4096, 2048], P('fsdp', 'seq')
- value_grad: bfloat16 [8, 4096, 2048], P('fsdp', 'seq')
- weight_grad: float32 [2048, 2048], P('seq', 'fsdp')
All inputs are finite; a program needn't handle non-finite values.
Results may differ from a plain program's by a relative error of at most 0.005.
Values may be sent and summed in bfloat16 or wider, within the bound.
A program may use at most 192 MiB of HBM per device.

v0:
```python
import math

import jax
import jax.numpy as jnp
from jax import lax
from jax.sharding import PartitionSpec as P

HEADS = 16
HEAD_DIM = 128
BLOCK = 128


def carried_in(value, axis, combine, identity, reverse):
    length, here = (lax.axis_size(axis), lax.axis_index(axis))
    everything = lax.all_gather(value, axis)
    start = jnp.broadcast_to(jnp.asarray(identity, value.dtype), value.shape)

    def lap(k, before):
        at = length - 1 - k if reverse else k
        reached = at > here if reverse else at < here
        new = combine(before, everything[at])
        return jnp.where(reached, new, before)

    return lax.fori_loop(0, length, lap, start)


def add_states(earlier, after_dev):
    return earlier + after_dev


def attend(queries, key_vectors, value_vectors, grads, factor):
    batches, tokens, head_count, head_width = queries.shape
    blocks = tokens // BLOCK
    shape_five = (batches, blocks, BLOCK, head_count, head_width)
    query_wide = queries.reshape(shape_five)
    keys_wide = key_vectors.reshape(shape_five)
    values_wide = value_vectors.reshape(shape_five)
    grads_wide = grads.reshape(shape_five)
    single = jnp.float32
    higher = lax.Precision.HIGH
    key_value = jnp.einsum(
        "bnshd,bnshe->bnhde", keys_wide, values_wide, preferred_element_type=single
    )
    query_cot = jnp.einsum(
        "bnthd,bnthe->bnhde", query_wide, grads_wide, preferred_element_type=single
    )
    key_value_dev = jnp.sum(key_value, 1)
    query_cot_dev = jnp.sum(query_cot, 1)
    nothing = jnp.zeros_like(key_value_dev)
    earlier = carried_in(key_value_dev, "seq", add_states, nothing, False)
    after_dev = carried_in(query_cot_dev, "seq", add_states, nothing, True)
    s_before = earlier[:, None] + jnp.cumsum(key_value, 1) - key_value
    g_after = after_dev[:, None] + query_cot_dev[:, None] - jnp.cumsum(query_cot, 1)
    row_index = lax.broadcasted_iota(jnp.int32, (BLOCK, BLOCK), 0)
    col_index = lax.broadcasted_iota(jnp.int32, (BLOCK, BLOCK), 1)
    causal = (row_index >= col_index).astype(jnp.float32)
    scores = jnp.einsum("bnthd,bnshd->bnhts", query_wide, keys_wide, preferred_element_type=single)
    scores = (scores * causal).astype(jnp.bfloat16)
    mixing = jnp.einsum(
        "bnthe,bnshe->bnhts", grads_wide, values_wide, preferred_element_type=single
    )
    mixing = (mixing * causal).astype(jnp.bfloat16)
    attended = jnp.einsum(
        "bnthd,bnhde->bnthe", query_wide.astype(single), s_before, precision=higher
    )
    attended = attended + jnp.einsum(
        "bnhts,bnshe->bnthe", scores, values_wide, preferred_element_type=single
    )
    query_grad = jnp.einsum(
        "bnthe,bnhde->bnthd", grads_wide.astype(single), s_before, precision=higher
    )
    query_grad = query_grad + jnp.einsum(
        "bnhts,bnshd->bnthd", mixing, keys_wide, preferred_element_type=single
    )
    key_grad = jnp.einsum(
        "bnshe,bnhde->bnshd", values_wide.astype(single), g_after, precision=higher
    )
    key_grad = key_grad + jnp.einsum(
        "bnhts,bnthd->bnshd", mixing, query_wide, preferred_element_type=single
    )
    value_grad = jnp.einsum(
        "bnshd,bnhde->bnshe", keys_wide.astype(single), g_after, precision=higher
    )
    value_grad = value_grad + jnp.einsum(
        "bnhts,bnthe->bnshe", scores, grads_wide, preferred_element_type=single
    )
    flat = (batches, tokens, head_count * head_width)
    return (
        factor * attended.reshape(flat),
        factor * query_grad.reshape(flat),
        factor * key_grad.reshape(flat),
        factor * value_grad.reshape(flat),
    )


def split_heads(values_in, head_count):
    return values_in.reshape(values_in.shape[0], values_in.shape[1], head_count, HEAD_DIM)


def body(queries, key_vectors, value_vectors, out_grad, out_weight):
    seq_devices = lax.axis_size("seq")
    fsdp_devices = lax.axis_size("fsdp")
    tokens = queries.shape[1]
    factor = 1.0 / math.sqrt(HEAD_DIM * tokens * seq_devices)
    grad_factor = 1.0 / math.sqrt(fsdp_devices * tokens * seq_devices)
    group_count = HEADS // fsdp_devices
    grads_all = lax.all_gather(out_grad, "fsdp", axis=0, tiled=True)
    grad_attn = jnp.einsum(
        "btd,dc->btc", grads_all, out_weight, preferred_element_type=jnp.float32
    ).astype(jnp.bfloat16)
    moved = (
        lax.all_to_all(queries, "fsdp", split_axis=2, concat_axis=0, tiled=True),
        lax.all_to_all(key_vectors, "fsdp", split_axis=2, concat_axis=0, tiled=True),
        lax.all_to_all(value_vectors, "fsdp", split_axis=2, concat_axis=0, tiled=True),
    )
    attended, query_grad, key_grad, value_grad = attend(
        split_heads(moved[0], group_count),
        split_heads(moved[1], group_count),
        split_heads(moved[2], group_count),
        split_heads(grad_attn, group_count),
        factor,
    )
    returned = (
        lax.all_to_all(
            query_grad.astype(jnp.bfloat16), "fsdp", split_axis=0, concat_axis=2, tiled=True
        ),
        lax.all_to_all(
            key_grad.astype(jnp.bfloat16), "fsdp", split_axis=0, concat_axis=2, tiled=True
        ),
        lax.all_to_all(
            value_grad.astype(jnp.bfloat16), "fsdp", split_axis=0, concat_axis=2, tiled=True
        ),
    )
    attended_low = attended.astype(jnp.bfloat16)
    weight_grad = (
        lax.psum_scatter(
            lax.dot_general(
                grads_all,
                attended_low,
                (((0, 1), (0, 1)), ((), ())),
                preferred_element_type=jnp.float32,
            ),
            "seq",
            scatter_dimension=0,
            tiled=True,
        )
        * grad_factor
    )
    return (returned[0], returned[1], returned[2], weight_grad)


def solution(mesh):
    in_specs = (
        P("fsdp", "seq", None),
        P("fsdp", "seq", None),
        P("fsdp", "seq", None),
        P("fsdp", "seq", None),
        P(None, "fsdp"),
    )
    out_specs = (
        P("fsdp", "seq", None),
        P("fsdp", "seq", None),
        P("fsdp", "seq", None),
        P("seq", "fsdp"),
    )
    return jax.shard_map(body, mesh=mesh, in_specs=in_specs, out_specs=out_specs, check_vma=False)
```

profile of v0, /device:TPU:1, one launch (start us, length us, event | category | flops | bytes accessed | tf_op | source)
XLA Modules:
  0.0 712.4 jit_solution(7374934269452240862)
XLA Ops:
  7.9 2.4 copy.72
  10.8 11.5 %reduce = bf16[2048,128]{1,0:T(8,128)(2,1)S(1)} reduce(bf16[2048,1,128]{2,1,0:T(2,128)(2,1)S(1)} %bitcast.143, bf16[]{:T(256)} %broadcast.48), dimensions={1}, to_apply=%bitcast.91.reduce_sub_computation | reduce | bytes 1048578
  23.2 5.9 all-to-all-start
  29.2 2.4 copy.73
  31.5 11.5 %reduce.1 = bf16[2048,128]{1,0:T(8,128)(2,1)S(1)} reduce(bf16[2048,1,128]{2,1,0:T(2,128)(2,1)S(1)} %bitcast.145, bf16[]{:T(256)} %broadcast.48), dimensions={1}, to_apply=%bitcast.93.reduce_sub_computation | reduce | bytes 1048578
  45.1 4.1 all-to-all-start.1
  50.0 15.0 %all-to-all-done.1 = bf16[8,2,16384]{2,1,0:T(2,128)(2,1)} async-done(((bf16[8,2,16384]{2,1,0:T(2,128)(2,1)}), bf16[8,2,16384]{2,1,0:T(2,128)(2,1)}, u32[]{:S(2)}, u32[]{:S(2)}) %all-to-all-start.1) | async-done | bytes 524320 | tf_op jit(solution)/shard_map/all_to_all | solution.py:114
  65.0 2.2 reshape.158
  70.6 11.5 %reduce.2 = bf16[2048,128]{1,0:T(8,128)(2,1)S(1)} reduce(bf16[2048,1,128]{2,1,0:T(2,128)(2,1)S(1)} %bitcast.144, bf16[]{:T(256)} %broadcast.48), dimensions={1}, to_apply=%bitcast.95.reduce_sub_computation | reduce | bytes 1048578
  82.3 18.0 %all_to_all.99 = bf16[8,2,16384]{2,1,0:T(2,128)(2,1)S(1)} all-to-all(bf16[8,2,16384]{2,1,0:T(2,128)(2,1)S(1)} %reshape.159), channel_id=1, replica_groups=mesh['seq'=32,'fsdp'=8] {'fsdp'}, dimensions={0} | all-to-all | bytes 1048576 | tf_op jit(solution)/shard_map/all_to_all | solution.py:112
  100.9 22.4 %all-gather.6.cloned.1.call-done = bf16[8,128,2048]{2,1,0:T(8,128)(2,1)} async-done(((bf16[1,128,2048]{2,1,0:T(8,128)(2,1)}), bf16[8,128,2048]{2,1,0:T(8,128)(2,1)}) %all-gather.6.cloned.1.call-update) | async-done | bytes 4194320 | tf_op jit(solution)/shard_map/all_gather | solution.py:107
  123.3 3.4 convolution_convert_fusion
  128.9 2.3 fusion.12
  131.3 2.3 fusion.11
  133.6 220.5 %all-gather.8.cloned.1.call-done = f32[256,2,128,128]{3,2,1,0:T(8,128)} async-done(((f32[8,2,128,128]{3,2,1,0:T(8,128)}), f32[256,2,128,128]{3,2,1,0:T(8,128)}) %all-gather.8.cloned.1.call-update) | async-done | bytes 33554448 | tf_op jit(solution)/shard_map/all_gather | solution.py:15
  354.1 52.0 %while.30 = (s32[]{:T(128)}, f32[8,2,128,128]{3,2,1,0:T(8,128)S(1)}, s32[]{:T(128)}, f32[32,8,2,128,128]{4,3,2,1,0:T(8,128)}, s32[]{:T(128)}, /*index=5*/s32[]{:T(128)}) while((s32[]{:T(128)}, f32[8,2,128,128]{3,2,1,0:T(8,128)S(1)}, s32[]{:T(128)}, f32[32,8,2,128,128]{4,3,2,1,0:T(8,128)}, s32[]{:T(128)}, /*index=5*/s32[]{:T(128)}) %tuple.92), condition=%wide.region_1.0_spmd.clone, body=%wide.region_0.0_spmd.clone.sunk | while | flops 786436 | bytes 3145821 | solution.py:24
  406.1 2.3 fusion.14
  410.1 2.6 convolution_bitcast_fusion
  412.8 2.9 copy.108
  417.5 2.5 fusion.7
  419.9 4.2 all-to-all-start.2
  424.8 160.2 %all-gather.10.cloned.1.call-done = f32[256,2,128,128]{3,2,1,0:T(8,128)} async-done(((f32[8,2,128,128]{3,2,1,0:T(8,128)}), f32[256,2,128,128]{3,2,1,0:T(8,128)}) %all-gather.10.cloned.1.call-update) | async-done | bytes 33554448 | tf_op jit(solution)/shard_map/all_gather | solution.py:15
  585.0 52.1 %while.31 = (s32[]{:T(128)}, f32[8,2,128,128]{3,2,1,0:T(8,128)S(1)}, s32[]{:T(128)}, f32[32,8,2,128,128]{4,3,2,1,0:T(8,128)}, s32[]{:T(128)}, /*index=5*/s32[]{:T(128)}, s32[]{:T(128)}, s32[]{:T(128)}) while((s32[]{:T(128)}, f32[8,2,128,128]{3,2,1,0:T(8,128)S(1)}, s32[]{:T(128)}, f32[32,8,2,128,128]{4,3,2,1,0:T(8,128)}, s32[]{:T(128)}, ...), condition=%wide.region_3.4_spmd.clone, body=%wide.region_2.3_spmd.clone.sunk | while | flops 786440 | bytes 3145883 | solution.py:24
  640.2 2.3 fusion.8
  642.5 4.5 all-to-all-start.5
  647.1 2.1 fusion.17
  649.2 2.1 fusion.10
  651.3 5.2 all-to-all-done.5
  656.5 3.5 all-to-all-start.4
  660.1 2.0 copy.105
  662.1 39.0 %reduce-scatter.4.cloned.1.call-done = f32[64,256]{1,0:T(8,128)} async-done(((f32[2048,256]{1,0:T(8,128)}), f32[64,256]{1,0:T(8,128)}) %reduce-scatter.4.cloned.1.call-update) | async-done | bytes 65552
  702.8 2.0 copy.107
  (122 shorter events, 123.3 us)
Async XLA Ops:
  7.2 116.1 %copy-start = (bf16[2048,256]{1,0:T(8,128)(2,1)S(1)}, bf16[2048,256]{1,0:T(8,128)(2,1)}, u32[]{:S(2)}) copy-start(bf16[2048,256]{1,0:T(8,128)(2,1)} %param.13) | copy-start | bytes 3145732
  7.2 116.1 %all-gather.6.cloned.1.call-start = ((), (), s32[]{:S(2)}) async-start(), calls=%async_computation.7 | async-start | bytes 4718592 | tf_op jit(solution)/shard_map/all_gather | solution.py:107
  23.2 21.9 %all-to-all-start = ((bf16[8,2,16384]{2,1,0:T(2,128)(2,1)}), bf16[8,2,16384]{2,1,0:T(2,128)(2,1)S(1)}, u32[]{:S(2)}, u32[]{:S(2)}) async-start(bf16[8,2,16384]{2,1,0:T(2,128)(2,1)} %reshape.155), calls=%async_computation | async-start | bytes 1048576 | tf_op jit(solution)/shard_map/all_to_all | solution.py:113
  45.1 19.9 %all-to-all-start.1 = ((bf16[8,2,16384]{2,1,0:T(2,128)(2,1)}), bf16[8,2,16384]{2,1,0:T(2,128)(2,1)}, u32[]{:S(2)}, u32[]{:S(2)}) async-start(bf16[8,2,16384]{2,1,0:T(2,128)(2,1)} %reshape.157), calls=%async_computation.1 | async-start | bytes 1048576 | tf_op jit(solution)/shard_map/all_to_all | solution.py:114
  49.3 304.8 %all-gather.8.cloned.1.call-start = ((), (), s32[]{:S(2)}) async-start(), calls=%async_computation.8 | async-start | bytes 34603008 | tf_op jit(solution)/shard_map/all_gather | solution.py:15
  49.9 19.9 %copy-start.9 = (bf16[1,128,2048]{2,1,0:T(8,128)(2,1)S(1)}, bf16[1,128,2048]{2,1,0:T(8,128)(2,1)}, u32[]{:S(2)}) copy-start(bf16[1,128,2048]{2,1,0:T(8,128)(2,1)} %param.9) | copy-start | bytes 1572868
  50.0 32.2 %copy-start.4 = (bf16[1,128,2048]{1,2,0:T(8,128)(2,1)}, bf16[1,128,2048]{1,2,0:T(8,128)(2,1)S(1)}, u32[]{:S(2)}) copy-start(bf16[1,128,2048]{1,2,0:T(8,128)(2,1)S(1)} %copy.110) | copy-start | bytes 1572868
  67.3 0.8 copy-start.2
  69.6 515.4 %all-gather.10.cloned.1.call-start = ((), (), s32[]{:S(2)}) async-start(), calls=%async_computation.9 | async-start | bytes 34603008 | tf_op jit(solution)/shard_map/all_gather | solution.py:15
  100.9 26.2 %copy-start.6 = (bf16[1,128,2048]{1,2,0:T(8,128)(2,1)}, bf16[1,128,2048]{1,2,0:T(8,128)(2,1)S(1)}, u32[]{:S(2)}) copy-start(bf16[1,128,2048]{1,2,0:T(8,128)(2,1)S(1)} %copy.112) | copy-start | bytes 1572868
  127.0 1.9 copy-start.8
  406.1 4.0 copy-start.10
  419.9 222.6 %all-to-all-start.2 = ((bf16[8,128,256]{1,2,0:T(8,128)(2,1)}), bf16[8,128,256]{1,2,0:T(8,128)(2,1)}, u32[]{:S(2)}, u32[]{:S(2)}) async-start(bf16[8,128,256]{1,2,0:T(8,128)(2,1)} %bitcast.11), calls=%async_computation.2 | async-start | bytes 1048576 | tf_op jit(solution)/shard_map/all_to_all | solution.py:124
  424.2 276.9 %reduce-scatter.4.cloned.1.call-start = ((), (), s32[]{:S(2)}) async-start(), calls=%async_computation.10 | async-start | bytes 2162688
  585.0 53.5 %copy-start.5 = (bf16[1,128,2048]{1,2,0:T(8,128)(2,1)S(1)}, bf16[1,128,2048]{1,2,0:T(8,128)(2,1)}, u32[]{:S(2)}) copy-start(bf16[1,128,2048]{1,2,0:T(8,128)(2,1)} %copy-done.4) | copy-start | bytes 1572868
  638.5 8.6 %copy-start.3 = (bf16[1,128,2048]{1,2,0:T(8,128)(2,1)S(1)}, bf16[1,128,2048]{1,2,0:T(8,128)(2,1)}, u32[]{:S(2)}) copy-start(bf16[1,128,2048]{1,2,0:T(8,128)(2,1)} %copy-done.2) | copy-start | bytes 1572868
  640.2 9.0 %copy-start.7 = (bf16[1,128,2048]{1,2,0:T(8,128)(2,1)S(1)}, bf16[1,128,2048]{1,2,0:T(8,128)(2,1)}, u32[]{:S(2)}) copy-start(bf16[1,128,2048]{1,2,0:T(8,128)(2,1)} %copy-done.6) | copy-start | bytes 1572868
  642.5 14.0 %all-to-all-start.5 = ((bf16[8,128,256]{1,2,0:T(8,128)(2,1)}), bf16[8,128,256]{1,2,0:T(8,128)(2,1)}, u32[]{:S(2)}, u32[]{:S(2)}) async-start(bf16[8,128,256]{1,2,0:T(8,128)(2,1)} %bitcast.146), calls=%async_computation.5 | async-start | bytes 1048576 | tf_op jit(solution)/shard_map/all_to_all | solution.py:130
  647.1 58.7 %copy-start.1 = (bf16[2048,256]{1,0:T(8,128)(2,1)S(1)}, bf16[2048,256]{1,0:T(8,128)(2,1)}, u32[]{:S(2)}) copy-start(bf16[2048,256]{1,0:T(8,128)(2,1)} %param.13) | copy-start | bytes 3145732
  656.5 48.3 %all-to-all-start.4 = ((bf16[8,128,256]{1,2,0:T(8,128)(2,1)}), bf16[8,128,256]{1,2,0:T(8,128)(2,1)S(1)}, u32[]{:S(2)}, u32[]{:S(2)}) async-start(bf16[8,128,256]{1,2,0:T(8,128)(2,1)} %bitcast.23), calls=%async_computation.4 | async-start | bytes 1048576 | tf_op jit(solution)/shard_map/all_to_all | solution.py:127
Sparse Core Ops, SparseCore 0:
  9.8 113.4 all-gather.5
  126.1 227.9 all-gather.7
  356.9 228.0 all-gather.9
  589.0 112.0 reduce-scatter.3
where the time goes:
time: 720 us; the launch traced here: 712 us
  waiting for transfers between devices  465 us (65%)
  other arithmetic  137 us (19%)
  matrix products  29.2 us (4%)
  local copies, waits for them, and re-layouts  24.8 us (3%)
  starting transfers between devices  22.9 us (3%)
  blocking collectives  18 us (2%)
  between operations  14.1 us (2%)
    all_gather x2, waiting for transfers between devices, carried_in(): everything = lax.all_gather(value, axis)  381 us
    select_n x64, other arithmetic, lap(): return jnp.where(reached, new, before)  102 us
    unnamed x5, waiting for transfers between devices  40 us
    unnamed x5, other arithmetic  34.6 us
    all_gather x1, waiting for transfers between devices, body(): grads_all = lax.all_gather(out_grad, 'fsdp', axis=0, tiled=True)  22.4 us
    all_to_all x1, blocking collectives, body(): lax.all_to_all(queries, 'fsdp', split_axis=2, concat_axis=0, tiled=True)  18 us
    unnamed x38, local copies, waits for them, and re-layouts  16.8 us
    all_to_all x1, waiting for transfers between devices, body(): lax.all_to_all(value_vectors, 'fsdp', split_axis=2, concat_axis=0, tiled=...  15 us
  transfers between devices with their start and end apart: 9, of which 7 were waited for; matrix products, arithmetic and copies ran while one was open for 27% of the time, Pallas kernels for 0%

commit v1 on v0

v1 whole, which is shorter than its diff:
```python
import functools
import math

import jax
import jax.numpy as jnp
from jax import lax
from jax.experimental import pallas as pl
from jax.experimental.pallas import tpu as pltpu
from jax.sharding import PartitionSpec as P

HEADS = 16
HEAD_DIM = 128
BLOCK = 128
MESH = pl.DeviceIdType.MESH
F32 = jnp.float32
BF16 = jnp.bfloat16
NT = (((1,), (1,)), ((), ()))
TN = (((0,), (0,)), ((), ()))


def dot(a, b, dims=(((1,), (0,)), ((), ()))):
    return lax.dot_general(a, b, dims, preferred_element_type=F32)


def head_cols(h):
    return pl.ds(pl.multiple_of(h * HEAD_DIM, HEAD_DIM), HEAD_DIM)


def kernel(
    chips,
    ring,
    factor,
    grad_factor,
    q_ref,
    k_ref,
    v_ref,
    og_ref,
    w_ref,
    qg_ref,
    kg_ref,
    vg_ref,
    wg_ref,
    og_all,
    gbuf,
    gsend,
    att_all,
    att_send,
    contrib,
    xc_send,
    xc_recv,
    a_send,
    a_recv,
    r_send,
    r_recv,
    p_out,
    state,
    acc_a,
    acc_k,
    acc_v,
    part,
    wx_send,
    wx_recv,
    wa_send,
    wa_recv,
    ag_ss,
    ag_rs,
    g_ss,
    g_rs,
    at_ss,
    at_rs,
    x_ss,
    x_rs,
    a_ss,
    a_rs,
):
    s = lax.axis_index("seq")
    f = lax.axis_index("fsdp")
    group = 2 * ring
    half = HEADS // 2
    chip, core = s // 2, s % 2
    mate = s + 1 - 2 * core
    yy, xl = f // 2, f % 2
    xp = f + 1 - 2 * xl
    up = ((yy + 1) % ring) * 2
    down = ((yy + ring - 1) % ring) * 2
    far = ((yy + 2) % ring) * 2
    ol = 1 - xl
    slice_rows = half * HEAD_DIM // chips

    def remote(src, dst, ssem, rsem, dev):
        return pltpu.make_async_remote_copy(
            src_ref=src,
            dst_ref=dst,
            send_sem=ssem,
            recv_sem=rsem,
            device_id=dev,
            device_id_type=MESH,
        )

    barrier = pltpu.get_barrier_semaphore()

    @pl.loop(1, group)
    def _(j):
        pl.semaphore_signal(barrier, inc=1, device_id=(s, (f + j) % group), device_id_type=MESH)

    @pl.loop(1, chips)
    def _(j):
        other = ((chip + j) % chips) * 2 + core
        pl.semaphore_signal(barrier, inc=1, device_id=(other, f), device_id_type=MESH)

    pl.semaphore_signal(barrier, inc=1, device_id=(mate, f), device_id_type=MESH)
    pl.semaphore_wait(barrier, group - 1 + chips - 1 + 1)

    def ag_full(n, slot, dev):
        return remote(og_all.at[slot], og_all.at[slot], ag_ss.at[n], ag_rs.at[slot, 0], (s, dev))

    def ag_own(n, dev):
        return remote(og_ref, og_all.at[f], ag_ss.at[n], ag_rs.at[f, 0], (s, dev))

    def ag_half(n, slot, part_at, dev):
        rows = pl.ds(part_at * (BLOCK // 2), BLOCK // 2)
        view = og_all.at[slot, rows]
        return remote(view, view, ag_ss.at[n], ag_rs.at[slot, part_at], (s, dev))

    ag_own(0, up + xl).start()
    ag_own(1, down + xl).start()
    ag_own(2, xp).start()

    def contrib_rows(b, left, right, first):
        @pl.loop(0, half // 2)
        def _(i):
            for u in range(2):
                h = first + 2 * i + u
                contrib[b, 2 * i + u] = dot(left(h), right(h), TN)

    def pair_start(b, left, right):
        other = (1 - core) * half

        @pl.loop(0, half // 2)
        def _(i):
            for u in range(2):
                h = other + 2 * i + u
                xc_send[b, 2 * i + u] = dot(left(h), right(h), TN).astype(BF16)

        remote(xc_send.at[b], xc_recv.at[b], x_ss.at[2 * b], x_rs.at[2 * b], (mate, f)).start()
        contrib_rows(b, left, right, core * half)

    def a2a_copy(src, dst, n, there):
        return remote(
            src, dst, a_ss.at[n, there], a_rs.at[n, chip], (there * 2 + core, f)
        )

    def a2a_start(src, dst, n):
        @pl.loop(1, chips)
        def _(j):
            there = (chip + j) % chips
            a2a_copy(src.at[there], dst.at[chip], n, there).start()

    def a2a_wait(src, dst, n):
        @pl.loop(1, chips)
        def _(j):
            there = (chip + j) % chips
            remote(
                src.at[there], dst.at[there], a_ss.at[n, there], a_rs.at[n, there],
                (there * 2 + core, f),
            ).wait_recv()

    def a2a_drain(src, dst, n):
        @pl.loop(1, chips)
        def _(j):
            there = (chip + j) % chips
            a2a_copy(src.at[there], dst.at[chip], n, there).wait_send()

    def sum_start(b):
        remote(xc_send.at[b], xc_recv.at[b], x_ss.at[2 * b], x_rs.at[2 * b], (mate, f)).wait_recv()

        @pl.loop(0, chips)
        def _(j):
            head, row = j * slice_rows // HEAD_DIM, pl.multiple_of((j * slice_rows) % HEAD_DIM, slice_rows)
            rows = pl.ds(row, slice_rows)
            total = contrib[b, head, rows] + xc_recv[b, head, rows].astype(F32)
            a_send[b, j] = total.astype(BF16)

        a_recv[b, chip] = a_send[b, chip]
        a2a_start(a_send.at[b], a_recv.at[b], 2 * b)

    def run_start(b, reverse):
        a2a_wait(a_send.at[b], a_recv.at[b], 2 * b)
        total = jnp.zeros((slice_rows, HEAD_DIM), F32)
        for j in range(chips):
            at = chips - 1 - j if reverse else j
            r_send[b, at] = total.astype(BF16)
            total = total + a_recv[b, at].astype(F32)
        r_recv[b, chip] = r_send[b, chip]
        a2a_start(r_send.at[b], r_recv.at[b], 2 * b + 1)

    def state_start(b, reverse):
        a2a_wait(r_send.at[b], r_recv.at[b], 2 * b + 1)
        first = core == (1 if reverse else 0)

        @pl.loop(0, chips)
        def _(j):
            head, row = j * slice_rows // HEAD_DIM, pl.multiple_of((j * slice_rows) % HEAD_DIM, slice_rows)
            rows = pl.ds(row, slice_rows)
            carried = r_recv[b, j].astype(F32)
            mine = contrib[b, head, rows]
            theirs = xc_recv[b, head, rows].astype(F32)
            p_out[b, head, rows] = (carried + jnp.where(first, mine, 0.0)).astype(BF16)
            state[b, core * half + head, rows] = (carried + jnp.where(first, 0.0, theirs)).astype(BF16)

        pair_state(b).start()

    def pair_state(b):
        heads = pl.ds(core * half, half)
        return remote(p_out.at[b], state.at[b, heads], x_ss.at[2 * b + 1], x_rs.at[2 * b + 1], (mate, f))

    def state_wait(b):
        heads = pl.ds((1 - core) * half, half)
        remote(p_out.at[b], state.at[b, heads], x_ss.at[2 * b + 1], x_rs.at[2 * b + 1], (mate, f)).wait_recv()

    def q_of(h):
        return q_ref[:, head_cols(h)]

    def k_of(h):
        return k_ref[:, head_cols(h)]

    def v_of(h):
        return v_ref[:, head_cols(h)]

    def g_of(h):
        return gbuf[h // 2, :, pl.ds(pl.multiple_of((h % 2) * HEAD_DIM, HEAD_DIM), HEAD_DIM)]

    pair_start(0, k_of, v_of)
    og_all[f] = og_ref[...]
    sum_start(0)

    def g_copy(slot):
        return remote(gsend.at[slot], gbuf.at[f], g_ss.at[slot], g_rs.at[f], (s, slot))

    def g_make(slot):
        gsend[slot] = dot(og_all[slot], w_ref[...]).astype(BF16)
        g_copy(slot).start()

    gbuf[f] = dot(og_ref[...], w_ref[...]).astype(BF16)

    row_index = lax.broadcasted_iota(jnp.int32, (BLOCK, BLOCK), 0)
    col_index = lax.broadcasted_iota(jnp.int32, (BLOCK, BLOCK), 1)
    lower = row_index >= col_index
    upper = row_index <= col_index

    @pl.loop(0, HEADS // 2)
    def _(i):
        for u in range(2):
            h = 2 * i + u
            scores = jnp.where(lower, dot(q_of(h), k_of(h), NT), 0.0).astype(BF16)
            acc_a[:, head_cols(h)] = dot(scores, v_of(h))

    ag_full(0, down + xl, f).wait_recv()
    ag_half(3, down + xl, 0, up + xl).start()
    ag_full(0, up + xl, f).wait_recv()
    ag_half(4, up + xl, 1, down + xl).start()
    ag_full(0, xp, f).wait_recv()
    ag_full(5, xp, up + xl).start()
    ag_full(6, xp, down + xl).start()
    g_make(down + xl)
    g_make(up + xl)
    g_make(xp)

    run_start(0, False)

    ag_half(0, far + xl, 0, f).wait_recv()
    ag_half(0, far + xl, 1, f).wait_recv()
    ag_full(7, far + xl, xp).start()
    g_make(far + xl)

    state_start(0, False)
    state_wait(0)

    def at_copy(slot):
        return remote(att_send.at[slot], att_all.at[f], at_ss.at[slot], at_rs.at[f], (s, slot))

    @pl.loop(0, HEADS // 2)
    def _(i):
        for u in range(2):
            h = 2 * i + u
            attended = dot(q_of(h), state[0, h]) + acc_a[:, head_cols(h)]
            att_send[i, :, u * HEAD_DIM:(u + 1) * HEAD_DIM] = (factor * attended).astype(BF16)

    att_all[f] = att_send[f]

    @pl.loop(1, group)
    def _(j):
        at_copy((f + j) % group).start()

    ag_full(0, down + ol, f).wait_recv()
    g_make(down + ol)
    ag_full(0, up + ol, f).wait_recv()
    g_make(up + ol)
    ag_full(0, far + ol, f).wait_recv()
    g_make(far + ol)

    @pl.loop(1, group)
    def _(j):
        slot = (f + j) % group
        remote(gsend.at[slot], gbuf.at[slot], g_ss.at[slot], g_rs.at[slot], (s, slot)).wait_recv()

    pair_start(1, q_of, g_of)
    sum_start(1)

    @pl.loop(0, HEADS // 2)
    def _(i):
        for u in range(2):
            h = 2 * i + u
            q, k, v, g = q_of(h), k_of(h), v_of(h), g_of(h)
            mixing = jnp.where(lower, dot(g, v, NT), 0.0).astype(BF16)
            grad = dot(mixing, k) + dot(g, state[0, h], NT)
            qg_ref[:, head_cols(h)] = (factor * grad).astype(BF16)
            mixing_t = jnp.where(upper, dot(v, g, NT), 0.0).astype(BF16)
            acc_k[:, head_cols(h)] = dot(mixing_t, q)
            scores_t = jnp.where(upper, dot(k, q, NT), 0.0).astype(BF16)
            acc_v[:, head_cols(h)] = dot(scores_t, g)

    run_start(1, True)

    @pl.loop(1, group)
    def _(j):
        slot = (f + j) % group
        remote(att_send.at[slot], att_all.at[slot], at_ss.at[slot], at_rs.at[slot], (s, slot)).wait_recv()

    depth, width = w_ref.shape
    out_rows = wg_ref.shape[0]
    step = 256
    rows_all = group * BLOCK

    @pl.loop(0, depth // step)
    def _(i):
        cols = pl.ds(pl.multiple_of(i * step, step), step)
        left = og_all[:, :, cols].reshape(rows_all, step)
        piece = dot(left, att_all[...].reshape(rows_all, width), TN)
        for n in range(step // (2 * out_rows)):
            at = i * (step // (2 * out_rows)) + n
            base = n * 2 * out_rows
            for c in range(2):
                rows = piece[base + c * out_rows:base + (c + 1) * out_rows]
                part[c, at] = rows

    @pl.loop(0, chips)
    def _(j):
        wx_send[j] = part[1 - core, j].astype(BF16)

    w_pair = remote(wx_send, wx_recv, x_ss.at[4], x_rs.at[4], (mate, f))
    w_pair.start()

    state_start(1, True)

    w_pair.wait_recv()

    @pl.loop(0, chips)
    def _(j):
        wa_send[j] = (part[core, j] + wx_recv[j].astype(F32)).astype(BF16)

    wa_recv[chip] = wa_send[chip]
    a2a_start(wa_send, wa_recv, 4)

    state_wait(1)

    @pl.loop(0, HEADS // 2)
    def _(i):
        for u in range(2):
            h = 2 * i + u
            after = state[1, h]
            grad = dot(v_of(h), after, NT) + acc_k[:, head_cols(h)]
            kg_ref[:, head_cols(h)] = (factor * grad).astype(BF16)
            grad = dot(k_of(h), after) + acc_v[:, head_cols(h)]
            vg_ref[:, head_cols(h)] = (factor * grad).astype(BF16)

    a2a_wait(wa_send, wa_recv, 4)
    total = wa_recv[0].astype(F32)
    for j in range(1, chips):
        total = total + wa_recv[j].astype(F32)
    wg_ref[...] = total * grad_factor

    ag_own(0, up + xl).wait_send()
    ag_own(1, down + xl).wait_send()
    ag_own(2, xp).wait_send()
    ag_half(3, down + xl, 0, up + xl).wait_send()
    ag_half(4, up + xl, 1, down + xl).wait_send()
    ag_full(5, xp, up + xl).wait_send()
    ag_full(6, xp, down + xl).wait_send()
    ag_full(7, far + xl, xp).wait_send()

    @pl.loop(1, group)
    def _(j):
        slot = (f + j) % group
        g_copy(slot).wait_send()
        at_copy(slot).wait_send()

    for b in range(2):
        remote(xc_send.at[b], xc_recv.at[b], x_ss.at[2 * b], x_rs.at[2 * b], (mate, f)).wait_send()
        pair_state(b).wait_send()
        a2a_drain(a_send.at[b], a_recv.at[b], 2 * b)
        a2a_drain(r_send.at[b], r_recv.at[b], 2 * b + 1)
    w_pair.wait_send()
    a2a_drain(wa_send, wa_recv, 4)


def body(queries, key_vectors, value_vectors, out_grad, out_weight):
    seq_devices = lax.axis_size("seq")
    group = lax.axis_size("fsdp")
    chips = seq_devices // 2
    _, tokens, width_all = queries.shape
    depth, width = out_weight.shape
    factor = 1.0 / math.sqrt(HEAD_DIM * tokens * seq_devices)
    grad_factor = 1.0 / math.sqrt(group * tokens * seq_devices)
    half = HEADS // 2
    out_rows = depth // seq_devices
    slice_rows = half * HEAD_DIM // chips
    flat = (tokens, width_all)
    vmem = pl.BlockSpec(memory_space=pltpu.VMEM)
    slices = pltpu.VMEM((2, chips, slice_rows, HEAD_DIM), BF16)
    half_low = pltpu.VMEM((2, half, HEAD_DIM, HEAD_DIM), BF16)
    pieces = pltpu.VMEM((chips, out_rows, width), BF16)
    blocks = pltpu.VMEM((group, tokens, width), BF16)
    dma = pltpu.SemaphoreType.DMA
    results = pl.pallas_call(
        functools.partial(kernel, chips, group // 2, factor, grad_factor),
        out_shape=(
            jax.ShapeDtypeStruct(flat, BF16),
            jax.ShapeDtypeStruct(flat, BF16),
            jax.ShapeDtypeStruct(flat, BF16),
            jax.ShapeDtypeStruct((out_rows, width), F32),
        ),
        in_specs=[vmem] * 5,
        out_specs=(vmem,) * 4,
        scratch_shapes=[
            pltpu.VMEM((group, tokens, depth), BF16),
            blocks,
            blocks,
            blocks,
            blocks,
            pltpu.VMEM((2, half, HEAD_DIM, HEAD_DIM), F32),
            half_low,
            half_low,
            slices,
            slices,
            slices,
            slices,
            half_low,
            pltpu.VMEM((2, HEADS, HEAD_DIM, HEAD_DIM), BF16),
            pltpu.VMEM(flat, F32),
            pltpu.VMEM(flat, F32),
            pltpu.VMEM(flat, F32),
            pltpu.VMEM((2, chips, out_rows, width), F32),
            pieces,
            pieces,
            pieces,
            pieces,
            dma((8,)),
            dma((group, 2)),
            dma((group,)),
            dma((group,)),
            dma((group,)),
            dma((group,)),
            dma((5,)),
            dma((5,)),
            dma((5, chips)),
            dma((5, chips)),
        ],
        compiler_params=pltpu.CompilerParams(
            collective_id=0, has_side_effects=True, vmem_limit_bytes=48 * 1024 * 1024
        ),
    )(
        queries.reshape(flat),
        key_vectors.reshape(flat),
        value_vectors.reshape(flat),
        out_grad.reshape(flat),
        out_weight,
    )
    whole = (1,) + flat
    return (
        results[0].reshape(whole),
        results[1].reshape(whole),
        results[2].reshape(whole),
        results[3],
    )


def solution(mesh):
    in_specs = (
        P("fsdp", "seq", None),
        P("fsdp", "seq", None),
        P("fsdp", "seq", None),
        P("fsdp", "seq", None),
        P(None, "fsdp"),
    )
    out_specs = (
        P("fsdp", "seq", None),
        P("fsdp", "seq", None),
        P("fsdp", "seq", None),
        P("seq", "fsdp"),
    )
    return jax.shard_map(body, mesh=mesh, in_specs=in_specs, out_specs=out_specs, check_vma=False)
```

time: 720 us -> 104 us (0.14)
  waiting for transfers between devices: 465 us -> 0 us
  other arithmetic: 137 us -> 0 us
  Pallas kernels: 0 us -> 93.1 us
  matrix products: 29.2 us -> 0 us
  starting transfers between devices: 22.9 us -> 0 us
  blocking collectives: 18 us -> 0 us
  local copies, waits for them, and re-layouts: 24.8 us -> 8.39 us
  between operations: 14.1 us -> 0.65 us
    all_gather x3 -> x0, waiting for transfers between devices: 403 us -> none  [the longest x2 381 us: carried_in(): everything = lax.all_gather(value, axis)]
    select_n x64 -> x0, other arithmetic: 102 us -> none  [lap(): return jnp.where(reached, new, before)]
    pallas_call x0 -> x1, Pallas kernels: none -> 93.1 us  [body(): pl.pallas_call(functools.partial(kernel, chips, group // 2, factor, grad_...]
    unnamed x5 -> x0, waiting for transfers between devices: 40 us -> none
    unnamed x5 -> x0, other arithmetic: 34.6 us -> none
    dot_general x14 -> x0, matrix products: 29.2 us -> none  [the longest x1 3.43 us: body(): jnp.einsum('btd,dc->btc', grads_all, out_weight, preferred_element_type=j...]
    all_to_all x5 -> x0, starting transfers between devices: 22.4 us -> none  [the longest x1 5.94 us: body(): lax.all_to_all(key_vectors, 'fsdp', split_axis=2, concat_axis=0, tiled=True)]
    all_to_all x5 -> x0, waiting for transfers between devices: 21.4 us -> none  [the longest x1 15 us: body(): lax.all_to_all(value_vectors, 'fsdp', split_axis=2, concat_axis=0, tiled=...]
  transfers between devices with their start and end apart: 9 -> 0, of which waited for: 7 -> 0; matrix products, arithmetic and copies ran while one was open for 27% -> 0% of each run, Pallas kernels for 0% -> 0%
where the time goes in v1:
time: 104 us; the launch traced here: 102 us
  Pallas kernels  93.1 us (90%)
  local copies, waits for them, and re-layouts  8.39 us (8%)
    pallas_call x1, Pallas kernels, body(): pl.pallas_call(functools.partial(kernel, chips, group // 2, factor, grad_...  93.1 us
    unnamed x14, local copies, waits for them, and re-layouts  8.39 us

profile of v1, /device:TPU:1, one launch (start us, length us, event | category | flops | bytes accessed | tf_op | source)
XLA Modules:
  0.0 102.1 jit_solution(3529953444678933017)
XLA Ops:
  0.6 0.0 copy-start
  0.6 1.2 %copy-done = bf16[2048,256]{1,0:T(8,128)(2,1)S(1)} copy-done((bf16[2048,256]{1,0:T(8,128)(2,1)S(1)}, bf16[2048,256]{1,0:T(8,128)(2,1)}, u32[]{:S(2)}) %copy-start) | copy-done | bytes 1048600
  1.9 0.0 copy-start.1
  1.9 1.0 %copy-done.1 = bf16[1,128,2048]{2,1,0:T(8,128)(2,1)S(1)} copy-done((bf16[1,128,2048]{2,1,0:T(8,128)(2,1)S(1)}, bf16[1,128,2048]{2,1,0:T(8,128)(2,1)}, u32[]{:S(2)}) %copy-start.1) | copy-done | bytes 524312
  2.9 0.0 copy-start.2
  2.9 1.0 %copy-done.2 = bf16[1,128,2048]{2,1,0:T(8,128)(2,1)S(1)} copy-done((bf16[1,128,2048]{2,1,0:T(8,128)(2,1)S(1)}, bf16[1,128,2048]{2,1,0:T(8,128)(2,1)}, u32[]{:S(2)}) %copy-start.2) | copy-done | bytes 524312
  3.9 0.0 copy-start.3
  3.9 1.0 %copy-done.3 = bf16[1,128,2048]{2,1,0:T(8,128)(2,1)S(1)} copy-done((bf16[1,128,2048]{2,1,0:T(8,128)(2,1)S(1)}, bf16[1,128,2048]{2,1,0:T(8,128)(2,1)}, u32[]{:S(2)}) %copy-start.3) | copy-done | bytes 524312
  5.0 0.0 copy-start.4
  5.0 1.0 %copy-done.4 = bf16[1,128,2048]{2,1,0:T(8,128)(2,1)S(1)} copy-done((bf16[1,128,2048]{2,1,0:T(8,128)(2,1)S(1)}, bf16[1,128,2048]{2,1,0:T(8,128)(2,1)}, u32[]{:S(2)}) %copy-start.4) | copy-done | bytes 524312
  6.0 93.1 %shard_map.84 = (bf16[128,2048]{1,0:T(8,128)(2,1)S(1)}, bf16[128,2048]{1,0:T(8,128)(2,1)S(1)}, bf16[128,2048]{1,0:T(8,128)(2,1)S(1)}, f32[64,256]{1,0:T(8,128)S(1)}) custom-call(bf16[128,2048]{1,0:T(8,128)(2,1)S(1)} %bitcast.10, bf16[128,2048]{1,0:T(8,128)(2,1)S(1)} %bitcast.11, bf16[128,2048]{1,0:T(8,128)(2,1)S(1)} %bitcast.12, ...), custom_call_target="tpu_custom_call" | custom-call | tf_op jit(solution)/shard_map/pallas_call | solution.py:425
  99.1 0.8 copy.13
  99.9 0.8 copy.14
  100.7 0.8 copy.15
  101.5 0.6 copy.16
Async XLA Ops:
  0.6 1.2 %copy-start = (bf16[2048,256]{1,0:T(8,128)(2,1)S(1)}, bf16[2048,256]{1,0:T(8,128)(2,1)}, u32[]{:S(2)}) copy-start(bf16[2048,256]{1,0:T(8,128)(2,1)} %w_ref.1) | copy-start | bytes 3145732
  1.9 1.0 %copy-start.1 = (bf16[1,128,2048]{2,1,0:T(8,128)(2,1)S(1)}, bf16[1,128,2048]{2,1,0:T(8,128)(2,1)}, u32[]{:S(2)}) copy-start(bf16[1,128,2048]{2,1,0:T(8,128)(2,1)} %param.5) | copy-start | bytes 1572868
  2.9 1.0 %copy-start.2 = (bf16[1,128,2048]{2,1,0:T(8,128)(2,1)S(1)}, bf16[1,128,2048]{2,1,0:T(8,128)(2,1)}, u32[]{:S(2)}) copy-start(bf16[1,128,2048]{2,1,0:T(8,128)(2,1)} %param.6) | copy-start | bytes 1572868
  3.9 1.0 %copy-start.3 = (bf16[1,128,2048]{2,1,0:T(8,128)(2,1)S(1)}, bf16[1,128,2048]{2,1,0:T(8,128)(2,1)}, u32[]{:S(2)}) copy-start(bf16[1,128,2048]{2,1,0:T(8,128)(2,1)} %param.7) | copy-start | bytes 1572868
  5.0 1.0 %copy-start.4 = (bf16[1,128,2048]{2,1,0:T(8,128)(2,1)S(1)}, bf16[1,128,2048]{2,1,0:T(8,128)(2,1)}, u32[]{:S(2)}) copy-start(bf16[1,128,2048]{2,1,0:T(8,128)(2,1)} %param.8) | copy-start | bytes 1572868

commit v2 on v1

v2 whole, which is shorter than its diff:
```python
import functools
import math

import jax
import jax.numpy as jnp
from jax import lax
from jax.experimental import pallas as pl
from jax.experimental.pallas import tpu as pltpu
from jax.sharding import PartitionSpec as P

HEADS = 16
HEAD_DIM = 128
BLOCK = 128
MESH = pl.DeviceIdType.MESH
F32 = jnp.float32
BF16 = jnp.bfloat16
NT = (((1,), (1,)), ((), ()))
TN = (((0,), (0,)), ((), ()))


def dot(a, b, dims=(((1,), (0,)), ((), ()))):
    return lax.dot_general(a, b, dims, preferred_element_type=F32)


def head_cols(h):
    return pl.ds(pl.multiple_of(h * HEAD_DIM, HEAD_DIM), HEAD_DIM)


def kernel(
    chips,
    ring,
    factor,
    grad_factor,
    q_in,
    k_in,
    v_in,
    og_in,
    w_in,
    qg_ref,
    kg_ref,
    vg_ref,
    wg_ref,
    q_ref,
    k_ref,
    v_ref,
    w_ref,
    og_all,
    gbuf,
    gsend,
    att_all,
    att_send,
    contrib0,
    xc_send0,
    xc_recv0,
    slices0,
    p_out0,
    contrib1,
    xc_send1,
    xc_recv1,
    slices1,
    p_out1,
    state,
    acc_a,
    acc_k,
    acc_v,
    part,
    wp_send,
    wp_recv,
    wx_send,
    wx_recv,
    wz_send,
    wz_recv,
    in_sem,
    ag_ss,
    ag_rs,
    g_ss,
    g_rs,
    at_ss,
    at_rs,
    x_ss,
    x_rs,
    a_ss,
    a_rs,
    w_ss,
    w_rs,
):
    s = lax.axis_index("seq")
    f = lax.axis_index("fsdp")
    group = 2 * ring
    half = HEADS // 2
    chip, core = s // 2, s % 2
    mate = s + 1 - 2 * core
    yy, xl = f // 2, f % 2
    xp = f + 1 - 2 * xl
    up = ((yy + 1) % ring) * 2
    down = ((yy + ring - 1) % ring) * 2
    far = ((yy + 2) % ring) * 2
    ol = 1 - xl

    def remote(src, dst, ssem, rsem, dev):
        return pltpu.make_async_remote_copy(
            src_ref=src,
            dst_ref=dst,
            send_sem=ssem,
            recv_sem=rsem,
            device_id=dev,
            device_id_type=MESH,
        )

    load_k = pltpu.make_async_copy(k_in, k_ref, in_sem.at[0])
    load_v = pltpu.make_async_copy(v_in, v_ref, in_sem.at[1])
    load_og = pltpu.make_async_copy(og_in, og_all.at[f], in_sem.at[2])
    load_w = pltpu.make_async_copy(w_in, w_ref, in_sem.at[3])
    load_q = pltpu.make_async_copy(q_in, q_ref, in_sem.at[4])
    for load in (load_k, load_v, load_og, load_w, load_q):
        load.start()
    barrier = pltpu.get_barrier_semaphore()

    @pl.loop(1, group)
    def _(j):
        pl.semaphore_signal(barrier, inc=1, device_id=(s, (f + j) % group), device_id_type=MESH)

    @pl.loop(1, chips)
    def _(j):
        other = ((chip + j) % chips) * 2 + core
        pl.semaphore_signal(barrier, inc=1, device_id=(other, f), device_id_type=MESH)

    pl.semaphore_signal(barrier, inc=1, device_id=(mate, f), device_id_type=MESH)
    pl.semaphore_wait(barrier, group - 1 + chips - 1 + 1)

    def half_view(ref, part_at):
        return ref.at[pl.ds(part_at * (BLOCK // 2), BLOCK // 2)]

    def ag_own(n, part_at, dev):
        return remote(
            half_view(og_in, part_at), half_view(og_all.at[f], part_at),
            ag_ss.at[n, part_at], ag_rs.at[f, part_at], (s, dev),
        )

    def ag_pass(n, slot, part_at, dev):
        view = half_view(og_all.at[slot], part_at)
        return remote(view, view, ag_ss.at[n, part_at], ag_rs.at[slot, part_at], (s, dev))

    def ag_wait(slot, part_at):
        ag_pass(0, slot, part_at, xp).wait_recv()

    for part_at in range(2):
        ag_own(0, part_at, up + xl).start()
        ag_own(1, 1 - part_at, down + xl).start()
        ag_own(2, part_at, xp).start()

    def q_of(h):
        return q_ref[:, head_cols(h)]

    def k_of(h):
        return k_ref[:, head_cols(h)]

    def v_of(h):
        return v_ref[:, head_cols(h)]

    def g_of(h):
        return gbuf[h // 2, :, pl.ds(pl.multiple_of((h % 2) * HEAD_DIM, HEAD_DIM), HEAD_DIM)]

    def a2a_copy(src, dst, n, there):
        return remote(src, dst, a_ss.at[n], a_rs.at[n], (there * 2 + core, f))

    def a2a_start(src, dst, n):
        @pl.loop(1, chips)
        def _(j):
            there = (chip + j) % chips
            a2a_copy(src.at[there], dst.at[chip], n, there).start()

    def a2a_all(src, dst, n):
        every = pl.ds(0, chips - 1)
        return remote(src.at[every], dst.at[every], a_ss.at[n], a_rs.at[n], (mate, f))

    def a2a_wait(src, dst, n):
        a2a_all(src, dst, n).wait_recv()

    def a2a_drain(src, dst, n):
        a2a_all(src, dst, n).wait_send()

    class Scan:
        def __init__(self, at, b, reverse, mine, other, left, right, bufs):
            self.at, self.b, self.reverse = at, b, reverse
            self.mine, self.other, self.left, self.right = mine, other, left, right
            self.contrib, self.xc_send, self.xc_recv, slices, self.p_out = bufs
            self.a_send, self.a_recv, self.r_send, self.r_recv = [slices.at[i] for i in range(4)]
            self.heads = self.contrib.shape[0]
            self.rows = self.heads * HEAD_DIM // chips

        def pair(self):
            return remote(
                self.xc_send, self.xc_recv, x_ss.at[2 * self.at], x_rs.at[2 * self.at], (mate, f)
            )

        def place(self, j):
            row = pl.multiple_of((j * self.rows) % HEAD_DIM, self.rows)
            return j * self.rows // HEAD_DIM, pl.ds(row, self.rows)

        def start(self):
            @pl.loop(0, self.heads // 2)
            def _(i):
                for u in range(2):
                    h = self.other + 2 * i + u
                    self.xc_send[2 * i + u] = dot(self.left(h), self.right(h), TN)

            self.pair().start()

            @pl.loop(0, self.heads // 2)
            def _(i):
                for u in range(2):
                    h = self.mine + 2 * i + u
                    self.contrib[2 * i + u] = dot(self.left(h), self.right(h), TN)

        def spread(self):
            self.pair().wait_recv()

            @pl.loop(0, chips)
            def _(j):
                head, rows = self.place(j)
                self.a_send[j] = (self.contrib[head, rows] + self.xc_recv[head, rows]).astype(BF16)

            self.a_recv[chip] = self.a_send[chip]
            a2a_start(self.a_send, self.a_recv, 2 * self.at)

        def run(self):
            a2a_wait(self.a_send, self.a_recv, 2 * self.at)
            total = jnp.zeros((self.rows, HEAD_DIM), F32)
            for j in range(chips):
                at = chips - 1 - j if self.reverse else j
                self.r_send[at] = total.astype(BF16)
                total = total + self.a_recv[at].astype(F32)
            self.r_recv[chip] = self.r_send[chip]
            a2a_start(self.r_send, self.r_recv, 2 * self.at + 1)

        def back(self):
            heads = pl.ds(self.mine, self.heads)
            return remote(
                self.p_out, state.at[self.b, heads],
                x_ss.at[2 * self.at + 1], x_rs.at[2 * self.at + 1], (mate, f),
            )

        def finish(self):
            a2a_wait(self.r_send, self.r_recv, 2 * self.at + 1)
            first = core == (1 if self.reverse else 0)

            @pl.loop(0, chips)
            def _(j):
                head, rows = self.place(j)
                carried = self.r_recv[j].astype(F32)
                mine, theirs = self.contrib[head, rows], self.xc_recv[head, rows]
                self.p_out[head, rows] = (carried + jnp.where(first, mine, 0.0)).astype(BF16)
                state[self.b, self.mine + head, rows] = (
                    carried + jnp.where(first, 0.0, theirs)
                ).astype(BF16)

            self.back().start()

        def wait(self):
            heads = pl.ds(self.other, self.heads)
            remote(
                self.p_out, state.at[self.b, heads],
                x_ss.at[2 * self.at + 1], x_rs.at[2 * self.at + 1], (mate, f),
            ).wait_recv()

        def drain(self):
            self.pair().wait_send()
            self.back().wait_send()
            a2a_drain(self.a_send, self.a_recv, 2 * self.at)
            a2a_drain(self.r_send, self.r_recv, 2 * self.at + 1)

    kv = Scan(
        0, 0, False, core * half, (1 - core) * half, k_of, v_of,
        (contrib0, xc_send0, xc_recv0, slices0, p_out0),
    )
    pairs = ((f, xp), (down + xl, up + xl), (down + ol, up + ol), (far + xl, far + ol))
    qg = []
    for n, (first, second) in enumerate(pairs):
        mine = 2 * (first + core * (second - first))
        other = 2 * (second + core * (first - second))
        bufs = tuple(ref.at[n] for ref in (contrib1, xc_send1, xc_recv1, slices1, p_out1))
        qg.append(Scan(1 + n, 1, True, mine, other, q_of, g_of, bufs))

    load_k.wait()
    load_v.wait()
    kv.start()
    kv.spread()

    def g_copy(slot):
        return remote(gsend.at[slot], gbuf.at[f], g_ss.at[slot], g_rs.at[f], (s, slot))

    def g_make(slot):
        gsend[slot] = dot(og_all[slot], w_ref[...]).astype(BF16)
        g_copy(slot).start()

    def g_wait(slot):
        remote(gsend.at[slot], gbuf.at[slot], g_ss.at[slot], g_rs.at[slot], (s, slot)).wait_recv()

    load_og.wait()
    load_w.wait()
    gbuf[f] = dot(og_all[f], w_ref[...]).astype(BF16)

    row_index = lax.broadcasted_iota(jnp.int32, (BLOCK, BLOCK), 0)
    col_index = lax.broadcasted_iota(jnp.int32, (BLOCK, BLOCK), 1)
    lower = row_index >= col_index
    upper = row_index <= col_index
    load_q.wait()

    @pl.loop(0, HEADS // 2)
    def _(i):
        for u in range(2):
            h = 2 * i + u
            scores = jnp.where(lower, dot(q_of(h), k_of(h), NT), 0.0).astype(BF16)
            acc_a[:, head_cols(h)] = dot(scores, v_of(h))

    ag_wait(down + xl, 0)
    ag_pass(3, down + xl, 0, up + xl).start()
    ag_wait(up + xl, 1)
    ag_pass(3, up + xl, 1, down + xl).start()
    ag_wait(xp, 0)
    ag_pass(4, xp, 0, up + xl).start()
    ag_pass(5, xp, 0, down + xl).start()
    ag_wait(xp, 1)
    ag_pass(4, xp, 1, up + xl).start()
    ag_pass(5, xp, 1, down + xl).start()
    g_make(xp)
    kv.run()
    ag_wait(down + xl, 1)
    g_make(down + xl)
    ag_wait(up + xl, 0)
    g_make(up + xl)
    ag_wait(far + xl, 0)
    ag_pass(6, far + xl, 0, xp).start()
    ag_wait(far + xl, 1)
    ag_pass(6, far + xl, 1, xp).start()
    g_make(far + xl)

    def local_grads(h):
        q, k, v, g = q_of(h), k_of(h), v_of(h), g_of(h)
        mixing = jnp.where(lower, dot(g, v, NT), 0.0).astype(BF16)
        grad = dot(mixing, k) + dot(g, state[0, h], NT)
        qg_ref[:, head_cols(h)] = (factor * grad).astype(BF16)
        mixing_t = jnp.where(upper, dot(v, g, NT), 0.0).astype(BF16)
        acc_k[:, head_cols(h)] = dot(mixing_t, q)
        scores_t = jnp.where(upper, dot(k, q, NT), 0.0).astype(BF16)
        acc_v[:, head_cols(h)] = dot(scores_t, g)

    def local_pair(n):
        for column in pairs[n]:
            for u in range(2):
                local_grads(2 * column + u)

    def at_copy(slot):
        return remote(att_send.at[slot], att_all.at[f], at_ss.at[0], at_rs.at[0], (s, slot))

    def at_all():
        every = pl.ds(0, group - 1)
        return remote(att_send.at[every], att_all.at[every], at_ss.at[0], at_rs.at[0], (mate, f))

    g_wait(xp)
    qg[0].start()
    qg[0].spread()
    kv.finish()
    kv.wait()
    @pl.loop(0, HEADS // 2)
    def _(i):
        for u in range(2):
            h = 2 * i + u
            attended = dot(q_of(h), state[0, h]) + acc_a[:, head_cols(h)]
            att_send[i, :, u * HEAD_DIM:(u + 1) * HEAD_DIM] = (factor * attended).astype(BF16)

    att_all[f] = att_send[f]

    @pl.loop(1, group)
    def _(j):
        at_copy((f + j) % group).start()

    local_pair(0)
    ag_wait(down + ol, 0)
    ag_wait(down + ol, 1)
    g_make(down + ol)
    ag_wait(up + ol, 0)
    ag_wait(up + ol, 1)
    g_make(up + ol)
    ag_wait(far + ol, 0)
    ag_wait(far + ol, 1)
    g_make(far + ol)
    qg[0].run()
    g_wait(down + xl)
    g_wait(up + xl)
    qg[1].start()
    qg[1].spread()
    local_pair(1)

    at_all().wait_recv()

    depth, width = w_ref.shape
    out_rows = wg_ref.shape[0]
    step = 256
    rows_all = group * BLOCK

    @pl.loop(0, depth // step)
    def _(i):
        cols = pl.ds(pl.multiple_of(i * step, step), step)
        left = og_all[:, :, cols].reshape(rows_all, step)
        piece = dot(left, att_all[...].reshape(rows_all, width), TN)
        for n in range(2):
            for c in range(2):
                base = (2 * n + c) * out_rows
                part[c, n, i] = piece[base:base + out_rows]

    levels = chips // 2
    z, xh = chip // 2, chip % 2
    across = (2 * z + 1 - xh) * 2 + core
    quarter = out_rows // 2

    def w_rows(p):
        return pl.ds(p * quarter, quarter)

    def w_pair(p):
        return remote(wp_send.at[p], wp_recv.at[p], w_ss.at[p], w_rs.at[p], (mate, f))

    def w_cross(p):
        return remote(wx_send.at[p], wx_recv.at[p], w_ss.at[2 + p], w_rs.at[2 + p], (across, f))

    def w_level(p, there):
        to = (2 * there + xh) * 2 + core
        return remote(wz_send.at[p, there], wz_recv.at[p, z], w_ss.at[4 + p], w_rs.at[4 + p], (to, f))

    def w_levels(p):
        every = pl.ds(0, levels - 1)
        return remote(
            wz_send.at[p, every], wz_recv.at[p, every], w_ss.at[4 + p], w_rs.at[4 + p], (mate, f)
        )

    def w_pair_start(p):
        @pl.loop(0, levels)
        def _(j):
            for n in range(2):
                wp_send[p, n, j] = part[1 - core, n, j, w_rows(p)].astype(BF16)

        w_pair(p).start()

    def w_cross_start(p):
        w_pair(p).wait_recv()

        @pl.loop(0, levels)
        def _(j):
            total = part[core, 1 - xh, j, w_rows(p)] + wp_recv[p, 1 - xh, j].astype(F32)
            wx_send[p, j] = total.astype(BF16)

        w_cross(p).start()

    def w_level_start(p):
        w_cross(p).wait_recv()

        @pl.loop(0, levels)
        def _(j):
            total = part[core, xh, j, w_rows(p)] + wp_recv[p, xh, j].astype(F32)
            wz_send[p, j] = (total + wx_recv[p, j].astype(F32)).astype(BF16)

        wz_recv[p, z] = wz_send[p, z]

        @pl.loop(1, levels)
        def _(j):
            w_level(p, (z + j) % levels).start()

    def w_finish(p):
        w_levels(p).wait_recv()
        total = wz_recv[p, 0].astype(F32)
        for j in range(1, levels):
            total = total + wz_recv[p, j].astype(F32)
        wg_ref[w_rows(p)] = total * grad_factor

    w_pair_start(0)
    w_pair_start(1)
    g_wait(down + ol)
    g_wait(up + ol)
    qg[2].start()
    w_cross_start(0)
    w_cross_start(1)
    qg[2].spread()
    g_wait(far + xl)
    g_wait(far + ol)
    qg[3].start()
    qg[3].spread()
    qg[1].run()
    local_pair(2)
    w_level_start(0)
    local_pair(3)
    qg[2].run()
    w_level_start(1)
    qg[3].run()

    def final_pair(n):
        for column in pairs[n]:
            for u in range(2):
                h = 2 * column + u
                after = state[1, h]
                grad = dot(v_of(h), after, NT) + acc_k[:, head_cols(h)]
                kg_ref[:, head_cols(h)] = (factor * grad).astype(BF16)
                grad = dot(k_of(h), after) + acc_v[:, head_cols(h)]
                vg_ref[:, head_cols(h)] = (factor * grad).astype(BF16)

    qg[0].finish()
    qg[1].finish()
    for n in range(2):
        qg[n].wait()
        final_pair(n)
    qg[2].finish()
    qg[3].finish()
    for n in range(2, 4):
        qg[n].wait()
        final_pair(n)

    for part_at in range(2):
        ag_own(0, part_at, up + xl).wait_send()
        ag_own(1, part_at, down + xl).wait_send()
        ag_own(2, part_at, xp).wait_send()
        for n in range(3, 7):
            ag_pass(n, xp, part_at, xp).wait_send()

    @pl.loop(1, group)
    def _(j):
        g_copy((f + j) % group).wait_send()

    at_all().wait_send()
    kv.drain()
    for scan in qg:
        scan.drain()
    for p in range(2):
        w_pair(p).wait_send()
        w_cross(p).wait_send()
    for p in range(2):
        w_finish(p)
        w_levels(p).wait_send()


def store(*refs):
    sems = refs[-1]
    copies = [pltpu.make_async_copy(refs[i], refs[4 + i], sems.at[i]) for i in range(4)]
    for copy in copies:
        copy.start()
    for copy in copies:
        copy.wait()


def body(queries, key_vectors, value_vectors, out_grad, out_weight):
    seq_devices = lax.axis_size("seq")
    group = lax.axis_size("fsdp")
    chips = seq_devices // 2
    _, tokens, width_all = queries.shape
    depth, width = out_weight.shape
    factor = 1.0 / math.sqrt(HEAD_DIM * tokens * seq_devices)
    grad_factor = 1.0 / math.sqrt(group * tokens * seq_devices)
    half = HEADS // 2
    out_rows = depth // seq_devices
    flat = (tokens, width_all)
    vmem = pl.BlockSpec(memory_space=pltpu.VMEM)
    levels = chips // 2
    pieces = (levels, out_rows // 2, width)
    blocks = pltpu.VMEM((group, tokens, width), BF16)
    square = (HEAD_DIM, HEAD_DIM)
    chunk = (4, 2)
    dma = pltpu.SemaphoreType.DMA
    shapes = (
        jax.ShapeDtypeStruct(flat, BF16),
        jax.ShapeDtypeStruct(flat, BF16),
        jax.ShapeDtypeStruct(flat, BF16),
        jax.ShapeDtypeStruct((out_rows, width), F32),
    )
    args = [x.reshape(flat) for x in (queries, key_vectors, value_vectors, out_grad)]
    args = [pltpu.with_memory_space_constraint(x, pltpu.HBM) for x in (*args, out_weight)]
    results = pl.pallas_call(
        functools.partial(kernel, chips, group // 2, factor, grad_factor),
        out_shape=shapes,
        in_specs=[pl.BlockSpec(memory_space=pltpu.HBM)] * 5,
        out_specs=(vmem,) * 4,
        scratch_shapes=[
            pltpu.VMEM(flat, BF16),
            pltpu.VMEM(flat, BF16),
            pltpu.VMEM(flat, BF16),
            pltpu.VMEM((depth, width), BF16),
            pltpu.VMEM((group, tokens, depth), BF16),
            blocks,
            blocks,
            blocks,
            blocks,
            pltpu.VMEM((half,) + square, F32),
            pltpu.VMEM((half,) + square, F32),
            pltpu.VMEM((half,) + square, F32),
            pltpu.VMEM((4, chips, half * HEAD_DIM // chips, HEAD_DIM), BF16),
            pltpu.VMEM((half,) + square, BF16),
            pltpu.VMEM(chunk + square, F32),
            pltpu.VMEM(chunk + square, F32),
            pltpu.VMEM(chunk + square, F32),
            pltpu.VMEM((4, 4, chips, 2 * HEAD_DIM // chips, HEAD_DIM), BF16),
            pltpu.VMEM(chunk + square, BF16),
            pltpu.VMEM((2, HEADS) + square, BF16),
            pltpu.VMEM(flat, F32),
            pltpu.VMEM(flat, F32),
            pltpu.VMEM(flat, F32),
            pltpu.VMEM((2, 2, levels, out_rows, width), F32),
            pltpu.VMEM((2, 2) + pieces, BF16),
            pltpu.VMEM((2, 2) + pieces, BF16),
            pltpu.VMEM((2,) + pieces, BF16),
            pltpu.VMEM((2,) + pieces, BF16),
            pltpu.VMEM((2,) + pieces, BF16),
            pltpu.VMEM((2,) + pieces, BF16),
            dma((5,)),
            dma((7, 2)),
            dma((group, 2)),
            dma((group,)),
            dma((group,)),
            dma((1,)),
            dma((1,)),
            dma((10,)),
            dma((10,)),
            dma((10,)),
            dma((10,)),
            dma((6,)),
            dma((6,)),
        ],
        compiler_params=pltpu.CompilerParams(
            collective_id=0, has_side_effects=True, vmem_limit_bytes=44 * 1024 * 1024
        ),
    )(*args)
    results = pl.pallas_call(
        store,
        out_shape=shapes,
        in_specs=[vmem] * 4,
        out_specs=(pl.BlockSpec(memory_space=pltpu.HBM),) * 4,
        scratch_shapes=[dma((4,))],
        compiler_params=pltpu.CompilerParams(vmem_limit_bytes=16 * 1024 * 1024),
    )(*results)
    whole = (1,) + flat
    return (
        results[0].reshape(whole),
        results[1].reshape(whole),
        results[2].reshape(whole),
        results[3],
    )


def solution(mesh):
    in_specs = (
        P("fsdp", "seq", None),
        P("fsdp", "seq", None),
        P("fsdp", "seq", None),
        P("fsdp", "seq", None),
        P(None, "fsdp"),
    )
    out_specs = (
        P("fsdp", "seq", None),
        P("fsdp", "seq", None),
        P("fsdp", "seq", None),
        P("seq", "fsdp"),
    )
    return jax.shard_map(body, mesh=mesh, in_specs=in_specs, out_specs=out_specs, check_vma=False)
```

time: 104 us -> 82.4 us (0.79); the launches traced: 102 us -> 82.3 us
  Pallas kernels: 93.1 us -> 81.7 us
  local copies, waits for them, and re-layouts: 8.39 us -> 0 us
    pallas_call x1, Pallas kernels: 93.1 us -> 80.5 us  [body(): pl.pallas_call(functools.partial(kernel, chips, group // 2, factor, grad_...]
    unnamed x14 -> x0, local copies, waits for them, and re-layouts: 8.39 us -> none
    pallas_call x0 -> x1, Pallas kernels: none -> 1.18 us  [body(): pl.pallas_call(store, out_shape=shapes, in_specs=[vmem] * 4, out_specs=(p...]
where the time goes in v2:
time: 82.4 us; the launch traced here: 82.3 us
  Pallas kernels  81.7 us (99%)
    pallas_call x1, Pallas kernels, body(): pl.pallas_call(functools.partial(kernel, chips, group // 2, factor, grad_...  80.5 us

profile of v2, /device:TPU:1, one launch (start us, length us, event | category | flops | bytes accessed | tf_op | source)
XLA Modules:
  0.0 82.3 jit_solution(13921916018634100212)
XLA Ops:
  0.6 80.5 %shard_map.84 = (bf16[128,2048]{1,0:T(8,128)(2,1)S(1)}, bf16[128,2048]{1,0:T(8,128)(2,1)S(1)}, bf16[128,2048]{1,0:T(8,128)(2,1)S(1)}, f32[64,256]{1,0:T(8,128)S(1)}) custom-call(bf16[128,2048]{1,0:T(8,128)(2,1)} %bitcast.7, bf16[128,2048]{1,0:T(8,128)(2,1)} %bitcast.8, bf16[128,2048]{1,0:T(8,128)(2,1)} %bitcast.9, bf16[128,2048]{1,0:T(8,128)(2,1)} %bitcast.10, ...), custom_call_target="tpu_custom_call" | custom-call | tf_op jit(solution)/shard_map/pallas_call | solution.py:575
  81.1 1.2 %shard_map.85 = (bf16[128,2048]{1,0:T(8,128)(2,1)}, bf16[128,2048]{1,0:T(8,128)(2,1)}, bf16[128,2048]{1,0:T(8,128)(2,1)}, f32[64,256]{1,0:T(8,128)}) custom-call(bf16[128,2048]{1,0:T(8,128)(2,1)S(1)} %get-tuple-element.12.refs_0_, bf16[128,2048]{1,0:T(8,128)(2,1)S(1)} %get-tuple-element.13.refs_1_, bf16[128,2048]{1,0:T(8,128)(2,1)S(1)} %get-tuple-element.14.refs_2_, ...), custom_call_target="tpu_custom_call" | custom-call | tf_op jit(solution)/shard_map/pallas_call | solution.py:629

commit v3 on v2

--- a/solution.py
+++ b/solution.py
@@ -43,7 +43,7 @@
     q_ref,
     k_ref,
     v_ref,
-    w_ref,
+    w_all,
     og_all,
     gbuf,
     gsend,
@@ -89,6 +89,9 @@
     group = 2 * ring
     half = HEADS // 2
     chip, core = s // 2, s % 2
+    levels = chips // 2
+    z, xh = chip // 2, chip % 2
+    across = (2 * z + 1 - xh) * 2 + core
     mate = s + 1 - 2 * core
     yy, xl = f // 2, f % 2
     xp = f + 1 - 2 * xl
@@ -110,7 +113,7 @@
     load_k = pltpu.make_async_copy(k_in, k_ref, in_sem.at[0])
     load_v = pltpu.make_async_copy(v_in, v_ref, in_sem.at[1])
     load_og = pltpu.make_async_copy(og_in, og_all.at[f], in_sem.at[2])
-    load_w = pltpu.make_async_copy(w_in, w_ref, in_sem.at[3])
+    load_w = pltpu.make_async_copy(w_in, w_all.at[xl], in_sem.at[3])
     load_q = pltpu.make_async_copy(q_in, q_ref, in_sem.at[4])
     for load in (load_k, load_v, load_og, load_w, load_q):
         load.start()
@@ -126,28 +129,51 @@
         pl.semaphore_signal(barrier, inc=1, device_id=(other, f), device_id_type=MESH)
 
     pl.semaphore_signal(barrier, inc=1, device_id=(mate, f), device_id_type=MESH)
-    pl.semaphore_wait(barrier, group - 1 + chips - 1 + 1)
-
-    def half_view(ref, part_at):
-        return ref.at[pl.ds(part_at * (BLOCK // 2), BLOCK // 2)]
+    pl.semaphore_signal(barrier, inc=1, device_id=(across, xp), device_id_type=MESH)
+    pl.semaphore_wait(barrier, group - 1 + chips - 1 + 2)
+
+    def quarter_view(ref, part_at):
+        return ref.at[pl.ds(part_at * (BLOCK // 4), BLOCK // 4)]
 
     def ag_own(n, part_at, dev):
         return remote(
-            half_view(og_in, part_at), half_view(og_all.at[f], part_at),
+            quarter_view(og_in, part_at), quarter_view(og_all.at[f], part_at),
             ag_ss.at[n, part_at], ag_rs.at[f, part_at], (s, dev),
         )
 
     def ag_pass(n, slot, part_at, dev):
-        view = half_view(og_all.at[slot], part_at)
+        view = quarter_view(og_all.at[slot], part_at)
         return remote(view, view, ag_ss.at[n, part_at], ag_rs.at[slot, part_at], (s, dev))
 
-    def ag_wait(slot, part_at):
-        ag_pass(0, slot, part_at, xp).wait_recv()
-
-    for part_at in range(2):
-        ag_own(0, part_at, up + xl).start()
-        ag_own(1, 1 - part_at, down + xl).start()
-        ag_own(2, part_at, xp).start()
+    def ag_wait(slot, *parts_at):
+        for part_at in parts_at:
+            ag_pass(0, slot, part_at, xp).wait_recv()
+
+    own = [ag_own(0, p, up + xl) for p in range(4)] + [ag_own(1, p, down + xl) for p in (3, 2, 1, 0)]
+    own_across = [ag_own(2, p, xp) for p in range(4)]
+    past_up = [ag_pass(3, down + xl, p, up + xl) for p in (0, 1)]
+    past_down = [ag_pass(3, up + xl, p, down + xl) for p in (3, 2)]
+    partner_up = {p: ag_pass(4, xp, p, up + xl) for p in (0, 1, 2)}
+    partner_down = {p: ag_pass(5, xp, p, down + xl) for p in (1, 2, 3)}
+    far_across = {p: ag_pass(6, far + xl, p, xp) for p in range(4)}
+    down_across = ag_pass(7, down + xl, 3, xp)
+    up_across = ag_pass(7, up + xl, 0, xp)
+
+    w_part = w_in.shape[0] // 2
+    w_rows_here = pl.ds(core * w_part, w_part)
+    w_rows_mate = pl.ds((1 - core) * w_part, w_part)
+    w_side = remote(
+        w_in.at[w_rows_here], w_all.at[xl, w_rows_here], w_ss.at[6], w_rs.at[6], (across, xp)
+    )
+    w_got = w_all.at[1 - xl, w_rows_here]
+    w_share = remote(w_got, w_got, w_ss.at[7], w_rs.at[7], (mate, f))
+
+    w_side.start()
+    for p in range(4):
+        own[p].start()
+        own[4 + p].start()
+        if p < 2:
+            own_across[p].start()
 
     def q_of(h):
         return q_ref[:, head_cols(h)]
@@ -274,7 +300,7 @@
         0, 0, False, core * half, (1 - core) * half, k_of, v_of,
         (contrib0, xc_send0, xc_recv0, slices0, p_out0),
     )
-    pairs = ((f, xp), (down + xl, up + xl), (down + ol, up + ol), (far + xl, far + ol))
+    pairs = tuple((row, row + 1) for row in (2 * yy, up, down, far))
     qg = []
     for n, (first, second) in enumerate(pairs):
         mine = 2 * (first + core * (second - first))
@@ -286,20 +312,20 @@
     load_v.wait()
     kv.start()
     kv.spread()
-
-    def g_copy(slot):
-        return remote(gsend.at[slot], gbuf.at[f], g_ss.at[slot], g_rs.at[f], (s, slot))
-
-    def g_make(slot):
-        gsend[slot] = dot(og_all[slot], w_ref[...]).astype(BF16)
-        g_copy(slot).start()
-
-    def g_wait(slot):
-        remote(gsend.at[slot], gbuf.at[slot], g_ss.at[slot], g_rs.at[slot], (s, slot)).wait_recv()
-
-    load_og.wait()
-    load_w.wait()
-    gbuf[f] = dot(og_all[f], w_ref[...]).astype(BF16)
+    own_across[2].start()
+    own_across[3].start()
+
+    def g_copy(n, row):
+        to = gbuf.at[pl.ds(2 * yy, 2)]
+        return remote(gsend.at[n], to, g_ss.at[n], g_rs.at[yy], (s, row + xl))
+
+    def g_make(n, row):
+        for c in range(2):
+            gsend[n, c] = dot(og_all[row + xl], w_all[c]).astype(BF16)
+
+    def g_wait(row):
+        at = gbuf.at[pl.ds(row, 2)]
+        remote(gsend.at[0], at, g_ss.at[0], g_rs.at[row // 2], (s, row + xl)).wait_recv()
 
     row_index = lax.broadcasted_iota(jnp.int32, (BLOCK, BLOCK), 0)
     col_index = lax.broadcasted_iota(jnp.int32, (BLOCK, BLOCK), 1)
@@ -314,27 +340,39 @@
             scores = jnp.where(lower, dot(q_of(h), k_of(h), NT), 0.0).astype(BF16)
             acc_a[:, head_cols(h)] = dot(scores, v_of(h))
 
-    ag_wait(down + xl, 0)
-    ag_pass(3, down + xl, 0, up + xl).start()
-    ag_wait(up + xl, 1)
-    ag_pass(3, up + xl, 1, down + xl).start()
-    ag_wait(xp, 0)
-    ag_pass(4, xp, 0, up + xl).start()
-    ag_pass(5, xp, 0, down + xl).start()
-    ag_wait(xp, 1)
-    ag_pass(4, xp, 1, up + xl).start()
-    ag_pass(5, xp, 1, down + xl).start()
-    g_make(xp)
+    for n in range(2):
+        ag_wait(down + xl, n)
+        past_up[n].start()
+        ag_wait(up + xl, 3 - n)
+        past_down[n].start()
     kv.run()
-    ag_wait(down + xl, 1)
-    g_make(down + xl)
-    ag_wait(up + xl, 0)
-    g_make(up + xl)
-    ag_wait(far + xl, 0)
-    ag_pass(6, far + xl, 0, xp).start()
-    ag_wait(far + xl, 1)
-    ag_pass(6, far + xl, 1, xp).start()
-    g_make(far + xl)
+    for p in range(4):
+        ag_wait(xp, p)
+        if p < 3:
+            partner_up[p].start()
+        if p > 0:
+            partner_down[p].start()
+    ag_wait(down + xl, 2, 3)
+    down_across.start()
+    ag_wait(up + xl, 1, 0)
+    up_across.start()
+    remote(
+        w_in.at[w_rows_here], w_got, w_ss.at[6], w_rs.at[6], (across, xp)
+    ).wait_recv()
+    w_share.start()
+    load_og.wait()
+    load_w.wait()
+    w_theirs = w_all.at[1 - xl, w_rows_mate]
+    remote(w_theirs, w_theirs, w_ss.at[7], w_rs.at[7], (mate, f)).wait_recv()
+    for c in range(2):
+        gbuf[2 * yy + c] = dot(og_all[f], w_all[c]).astype(BF16)
+    g_make(0, up)
+    g_copy(0, up).start()
+    g_make(1, down)
+    g_copy(1, down).start()
+    for p in (0, 3, 1, 2):
+        ag_wait(far + xl, p)
+        far_across[p].start()
 
     def local_grads(h):
         q, k, v, g = q_of(h), k_of(h), v_of(h), g_of(h)
@@ -358,7 +396,6 @@
         every = pl.ds(0, group - 1)
         return remote(att_send.at[every], att_all.at[every], at_ss.at[0], at_rs.at[0], (mate, f))
 
-    g_wait(xp)
     qg[0].start()
     qg[0].spread()
     kv.finish()
@@ -376,47 +413,44 @@
     def _(j):
         at_copy((f + j) % group).start()
 
+    g_make(2, far)
+    g_copy(2, far).start()
     local_pair(0)
-    ag_wait(down + ol, 0)
-    ag_wait(down + ol, 1)
-    g_make(down + ol)
-    ag_wait(up + ol, 0)
-    ag_wait(up + ol, 1)
-    g_make(up + ol)
-    ag_wait(far + ol, 0)
-    ag_wait(far + ol, 1)
-    g_make(far + ol)
-    qg[0].run()
-    g_wait(down + xl)
-    g_wait(up + xl)
+    g_wait(up)
     qg[1].start()
     qg[1].spread()
     local_pair(1)
+    g_wait(down)
+    qg[2].start()
+    qg[2].spread()
+    local_pair(2)
+    g_wait(far)
+    qg[3].start()
+    qg[3].spread()
+    qg[0].run()
+    local_pair(3)
+    for row in (down, up, far):
+        ag_wait(row + ol, 0, 1, 2, 3)
 
     at_all().wait_recv()
 
-    depth, width = w_ref.shape
+    depth, width = w_in.shape
     out_rows = wg_ref.shape[0]
     step = 256
     rows_all = group * BLOCK
 
-    @pl.loop(0, depth // step)
-    def _(i):
-        cols = pl.ds(pl.multiple_of(i * step, step), step)
-        left = og_all[:, :, cols].reshape(rows_all, step)
-        piece = dot(left, att_all[...].reshape(rows_all, width), TN)
-        for n in range(2):
-            for c in range(2):
-                base = (2 * n + c) * out_rows
-                part[c, n, i] = piece[base:base + out_rows]
-
-    levels = chips // 2
-    z, xh = chip // 2, chip % 2
-    across = (2 * z + 1 - xh) * 2 + core
-    quarter = out_rows // 2
-
-    def w_rows(p):
-        return pl.ds(p * quarter, quarter)
+    pairs_of_levels = levels // 2
+
+    def w_part(p):
+        @pl.loop(0, pairs_of_levels)
+        def _(m):
+            cols = pl.ds(pl.multiple_of((2 * m + p) * step, step), step)
+            left = og_all[:, :, cols].reshape(rows_all, step)
+            piece = dot(left, att_all[...].reshape(rows_all, width), TN)
+            for n in range(2):
+                for c in range(2):
+                    base = (2 * n + c) * out_rows
+                    part[c, n, p, m] = piece[base:base + out_rows]
 
     def w_pair(p):
         return remote(wp_send.at[p], wp_recv.at[p], w_ss.at[p], w_rs.at[p], (mate, f))
@@ -424,74 +458,63 @@
     def w_cross(p):
         return remote(wx_send.at[p], wx_recv.at[p], w_ss.at[2 + p], w_rs.at[2 + p], (across, f))
 
-    def w_level(p, there):
-        to = (2 * there + xh) * 2 + core
-        return remote(wz_send.at[p, there], wz_recv.at[p, z], w_ss.at[4 + p], w_rs.at[4 + p], (to, f))
-
-    def w_levels(p):
-        every = pl.ds(0, levels - 1)
-        return remote(
-            wz_send.at[p, every], wz_recv.at[p, every], w_ss.at[4 + p], w_rs.at[4 + p], (mate, f)
-        )
+    def w_level(p, m):
+        to = (2 * (2 * m + p) + xh) * 2 + core
+        return remote(wz_send.at[p, m], wz_recv.at[z], w_ss.at[4], w_rs.at[4], (to, f))
+
+    def w_levels():
+        every = wz_recv.at[pl.ds(0, levels - 1)]
+        return remote(every, every, w_ss.at[4], w_rs.at[4], (mate, f))
 
     def w_pair_start(p):
-        @pl.loop(0, levels)
-        def _(j):
+        @pl.loop(0, pairs_of_levels)
+        def _(m):
             for n in range(2):
-                wp_send[p, n, j] = part[1 - core, n, j, w_rows(p)].astype(BF16)
+                wp_send[p, n, m] = part[1 - core, n, p, m].astype(BF16)
 
         w_pair(p).start()
 
     def w_cross_start(p):
         w_pair(p).wait_recv()
 
-        @pl.loop(0, levels)
-        def _(j):
-            total = part[core, 1 - xh, j, w_rows(p)] + wp_recv[p, 1 - xh, j].astype(F32)
-            wx_send[p, j] = total.astype(BF16)
+        @pl.loop(0, pairs_of_levels)
+        def _(m):
+            total = part[core, 1 - xh, p, m] + wp_recv[p, 1 - xh, m].astype(F32)
+            wx_send[p, m] = total.astype(BF16)
 
         w_cross(p).start()
 
     def w_level_start(p):
         w_cross(p).wait_recv()
 
-        @pl.loop(0, levels)
+        @pl.loop(0, pairs_of_levels)
+        def _(m):
+            total = part[core, xh, p, m] + wp_recv[p, xh, m].astype(F32)
+            wz_send[p, m] = (total + wx_recv[p, m].astype(F32)).astype(BF16)
+
+        @pl.when(z % 2 == p)
+        def _():
+            wz_recv[z] = wz_send[p, z // 2]
+
+        @pl.loop(0, pairs_of_levels)
         def _(j):
-            total = part[core, xh, j, w_rows(p)] + wp_recv[p, xh, j].astype(F32)
-            wz_send[p, j] = (total + wx_recv[p, j].astype(F32)).astype(BF16)
-
-        wz_recv[p, z] = wz_send[p, z]
-
-        @pl.loop(1, levels)
-        def _(j):
-            w_level(p, (z + j) % levels).start()
-
-    def w_finish(p):
-        w_levels(p).wait_recv()
-        total = wz_recv[p, 0].astype(F32)
-        for j in range(1, levels):
-            total = total + wz_recv[p, j].astype(F32)
-        wg_ref[w_rows(p)] = total * grad_factor
-
+            m = (z // 2 + j) % pairs_of_levels
+
+            @pl.when(2 * m + p != z)
+            def _():
+                w_level(p, m).start()
+
+    w_part(0)
     w_pair_start(0)
+    w_part(1)
     w_pair_start(1)
-    g_wait(down + ol)
-    g_wait(up + ol)
-    qg[2].start()
+    qg[1].run()
     w_cross_start(0)
+    qg[2].run()
+    qg[3].run()
     w_cross_start(1)
-    qg[2].spread()
-    g_wait(far + xl)
-    g_wait(far + ol)
-    qg[3].start()
-    qg[3].spread()
-    qg[1].run()
-    local_pair(2)
+    qg[0].finish()
     w_level_start(0)
-    local_pair(3)
-    qg[2].run()
-    w_level_start(1)
-    qg[3].run()
 
     def final_pair(n):
         for column in pairs[n]:
@@ -503,28 +526,23 @@
                 grad = dot(k_of(h), after) + acc_v[:, head_cols(h)]
                 vg_ref[:, head_cols(h)] = (factor * grad).astype(BF16)
 
-    qg[0].finish()
-    qg[1].finish()
-    for n in range(2):
+    for n in range(1, 3):
+        qg[n].finish()
+    for n in range(3):
         qg[n].wait()
         final_pair(n)
-    qg[2].finish()
+    w_level_start(1)
     qg[3].finish()
-    for n in range(2, 4):
-        qg[n].wait()
-        final_pair(n)
-
-    for part_at in range(2):
-        ag_own(0, part_at, up + xl).wait_send()
-        ag_own(1, part_at, down + xl).wait_send()
-        ag_own(2, part_at, xp).wait_send()
-        for n in range(3, 7):
-            ag_pass(n, xp, part_at, xp).wait_send()
-
-    @pl.loop(1, group)
-    def _(j):
-        g_copy((f + j) % group).wait_send()
-
+    qg[3].wait()
+    final_pair(3)
+    passed = [*own, *own_across, *past_up, *past_down, *partner_up.values(), *partner_down.values()]
+    for copy in (*passed, *far_across.values(), down_across, up_across):
+        copy.wait_send()
+
+    for n, row in enumerate((up, down, far)):
+        g_copy(n, row).wait_send()
+    w_side.wait_send()
+    w_share.wait_send()
     at_all().wait_send()
     kv.drain()
     for scan in qg:
@@ -532,9 +550,12 @@
     for p in range(2):
         w_pair(p).wait_send()
         w_cross(p).wait_send()
-    for p in range(2):
-        w_finish(p)
-        w_levels(p).wait_send()
+    w_levels().wait_recv()
+    total = wz_recv[0].astype(F32)
+    for j in range(1, levels):
+        total = total + wz_recv[j].astype(F32)
+    wg_ref[...] = total * grad_factor
+    w_levels().wait_send()
 
 
 def store(*refs):
@@ -559,7 +580,7 @@
     flat = (tokens, width_all)
     vmem = pl.BlockSpec(memory_space=pltpu.VMEM)
     levels = chips // 2
-    pieces = (levels, out_rows // 2, width)
+    pieces = (levels // 2, out_rows, width)
     blocks = pltpu.VMEM((group, tokens, width), BF16)
     square = (HEAD_DIM, HEAD_DIM)
     chunk = (4, 2)
@@ -581,10 +602,10 @@
             pltpu.VMEM(flat, BF16),
             pltpu.VMEM(flat, BF16),
             pltpu.VMEM(flat, BF16),
-            pltpu.VMEM((depth, width), BF16),
+            pltpu.VMEM((2, depth, width), BF16),
             pltpu.VMEM((group, tokens, depth), BF16),
             blocks,
-            blocks,
+            pltpu.VMEM((3, 2, tokens, width), BF16),
             blocks,
             blocks,
             pltpu.VMEM((half,) + square, F32),
@@ -601,26 +622,26 @@
             pltpu.VMEM(flat, F32),
             pltpu.VMEM(flat, F32),
             pltpu.VMEM(flat, F32),
-            pltpu.VMEM((2, 2, levels, out_rows, width), F32),
+            pltpu.VMEM((2, 2, 2, levels // 2, out_rows, width), F32),
             pltpu.VMEM((2, 2) + pieces, BF16),
             pltpu.VMEM((2, 2) + pieces, BF16),
             pltpu.VMEM((2,) + pieces, BF16),
             pltpu.VMEM((2,) + pieces, BF16),
             pltpu.VMEM((2,) + pieces, BF16),
-            pltpu.VMEM((2,) + pieces, BF16),
+            pltpu.VMEM((levels, out_rows, width), BF16),
             dma((5,)),
-            dma((7, 2)),
-            dma((group, 2)),
-            dma((group,)),
-            dma((group,)),
+            dma((8, 4)),
+            dma((group, 4)),
+            dma((3,)),
+            dma((group // 2,)),
             dma((1,)),
             dma((1,)),
             dma((10,)),
             dma((10,)),
             dma((10,)),
             dma((10,)),
-            dma((6,)),
-            dma((6,)),
+            dma((8,)),
+            dma((8,)),
         ],
         compiler_params=pltpu.CompilerParams(
             collective_id=0, has_side_effects=True, vmem_limit_bytes=44 * 1024 * 1024

time: 82.4 us -> 77.3 us (0.938)
  the two profiles are of different devices: /device:TPU:1 before, /device:TPU:39 now
where the time goes in v3:
time: 77.3 us; the launch traced here: 77.2 us
  Pallas kernels  76.6 us (99%)
    pallas_call x1, Pallas kernels, body(): pl.pallas_call(functools.partial(kernel, chips, group // 2, factor, grad_...  75.4 us

profile of v3, /device:TPU:39, one launch (start us, length us, event | category | flops | bytes accessed | tf_op | source)
XLA Modules:
  0.0 77.2 jit_solution(11831554157333432058)
XLA Ops:
  0.6 75.4 %shard_map.84 = (bf16[128,2048]{1,0:T(8,128)(2,1)S(1)}, bf16[128,2048]{1,0:T(8,128)(2,1)S(1)}, bf16[128,2048]{1,0:T(8,128)(2,1)S(1)}, f32[64,256]{1,0:T(8,128)S(1)}) custom-call(bf16[128,2048]{1,0:T(8,128)(2,1)} %bitcast.7, bf16[128,2048]{1,0:T(8,128)(2,1)} %bitcast.8, bf16[128,2048]{1,0:T(8,128)(2,1)} %bitcast.9, bf16[128,2048]{1,0:T(8,128)(2,1)} %bitcast.10, ...), custom_call_target="tpu_custom_call" | custom-call | tf_op jit(solution)/shard_map/pallas_call | solution.py:596
  76.0 1.2 %shard_map.85 = (bf16[128,2048]{1,0:T(8,128)(2,1)}, bf16[128,2048]{1,0:T(8,128)(2,1)}, bf16[128,2048]{1,0:T(8,128)(2,1)}, f32[64,256]{1,0:T(8,128)}) custom-call(bf16[128,2048]{1,0:T(8,128)(2,1)S(1)} %get-tuple-element.12.refs_0_, bf16[128,2048]{1,0:T(8,128)(2,1)S(1)} %get-tuple-element.13.refs_1_, bf16[128,2048]{1,0:T(8,128)(2,1)S(1)} %get-tuple-element.14.refs_2_, ...), custom_call_target="tpu_custom_call" | custom-call | tf_op jit(solution)/shard_map/pallas_call | solution.py:650

commit v4 on v3

--- a/solution.py
+++ b/solution.py
@@ -112,16 +112,17 @@
 
     load_k = pltpu.make_async_copy(k_in, k_ref, in_sem.at[0])
     load_v = pltpu.make_async_copy(v_in, v_ref, in_sem.at[1])
-    load_og = pltpu.make_async_copy(og_in, og_all.at[f], in_sem.at[2])
+    load_og = pltpu.make_async_copy(og_in, og_all.at[yy], in_sem.at[2])
     load_w = pltpu.make_async_copy(w_in, w_all.at[xl], in_sem.at[3])
     load_q = pltpu.make_async_copy(q_in, q_ref, in_sem.at[4])
     for load in (load_k, load_v, load_og, load_w, load_q):
         load.start()
     barrier = pltpu.get_barrier_semaphore()
 
-    @pl.loop(1, group)
+    @pl.loop(1, ring)
     def _(j):
-        pl.semaphore_signal(barrier, inc=1, device_id=(s, (f + j) % group), device_id_type=MESH)
+        row = (2 * yy + 2 * j) % group
+        pl.semaphore_signal(barrier, inc=1, device_id=(s, row + xl), device_id_type=MESH)
 
     @pl.loop(1, chips)
     def _(j):
@@ -130,15 +131,16 @@
 
     pl.semaphore_signal(barrier, inc=1, device_id=(mate, f), device_id_type=MESH)
     pl.semaphore_signal(barrier, inc=1, device_id=(across, xp), device_id_type=MESH)
-    pl.semaphore_wait(barrier, group - 1 + chips - 1 + 2)
+    pl.semaphore_signal(barrier, inc=1, device_id=(s, xp), device_id_type=MESH)
+    pl.semaphore_wait(barrier, ring - 1 + chips - 1 + 3)
 
     def quarter_view(ref, part_at):
         return ref.at[pl.ds(part_at * (BLOCK // 4), BLOCK // 4)]
 
     def ag_own(n, part_at, dev):
         return remote(
-            quarter_view(og_in, part_at), quarter_view(og_all.at[f], part_at),
-            ag_ss.at[n, part_at], ag_rs.at[f, part_at], (s, dev),
+            quarter_view(og_in, part_at), quarter_view(og_all.at[yy], part_at),
+            ag_ss.at[n, part_at], ag_rs.at[yy, part_at], (s, dev),
         )
 
     def ag_pass(n, slot, part_at, dev):
@@ -150,30 +152,22 @@
             ag_pass(0, slot, part_at, xp).wait_recv()
 
     own = [ag_own(0, p, up + xl) for p in range(4)] + [ag_own(1, p, down + xl) for p in (3, 2, 1, 0)]
-    own_across = [ag_own(2, p, xp) for p in range(4)]
-    past_up = [ag_pass(3, down + xl, p, up + xl) for p in (0, 1)]
-    past_down = [ag_pass(3, up + xl, p, down + xl) for p in (3, 2)]
-    partner_up = {p: ag_pass(4, xp, p, up + xl) for p in (0, 1, 2)}
-    partner_down = {p: ag_pass(5, xp, p, down + xl) for p in (1, 2, 3)}
-    far_across = {p: ag_pass(6, far + xl, p, xp) for p in range(4)}
-    down_across = ag_pass(7, down + xl, 3, xp)
-    up_across = ag_pass(7, up + xl, 0, xp)
+    past_up = [ag_pass(2, down // 2, p, up + xl) for p in (0, 1)]
+    past_down = [ag_pass(2, up // 2, p, down + xl) for p in (3, 2)]
 
     w_part = w_in.shape[0] // 2
     w_rows_here = pl.ds(core * w_part, w_part)
     w_rows_mate = pl.ds((1 - core) * w_part, w_part)
     w_side = remote(
-        w_in.at[w_rows_here], w_all.at[xl, w_rows_here], w_ss.at[6], w_rs.at[6], (across, xp)
+        w_in.at[w_rows_here], w_all.at[xl, w_rows_here], w_ss.at[9], w_rs.at[9], (across, xp)
     )
     w_got = w_all.at[1 - xl, w_rows_here]
-    w_share = remote(w_got, w_got, w_ss.at[7], w_rs.at[7], (mate, f))
+    w_share = remote(w_got, w_got, w_ss.at[10], w_rs.at[10], (mate, f))
 
     w_side.start()
     for p in range(4):
         own[p].start()
         own[4 + p].start()
-        if p < 2:
-            own_across[p].start()
 
     def q_of(h):
         return q_ref[:, head_cols(h)]
@@ -312,8 +306,6 @@
     load_v.wait()
     kv.start()
     kv.spread()
-    own_across[2].start()
-    own_across[3].start()
 
     def g_copy(n, row):
         to = gbuf.at[pl.ds(2 * yy, 2)]
@@ -321,7 +313,7 @@
 
     def g_make(n, row):
         for c in range(2):
-            gsend[n, c] = dot(og_all[row + xl], w_all[c]).astype(BF16)
+            gsend[n, c] = dot(og_all[row // 2], w_all[c]).astype(BF16)
 
     def g_wait(row):
         at = gbuf.at[pl.ds(row, 2)]
@@ -341,38 +333,27 @@
             acc_a[:, head_cols(h)] = dot(scores, v_of(h))
 
     for n in range(2):
-        ag_wait(down + xl, n)
+        ag_wait(down // 2, n)
         past_up[n].start()
-        ag_wait(up + xl, 3 - n)
+        ag_wait(up // 2, 3 - n)
         past_down[n].start()
     kv.run()
-    for p in range(4):
-        ag_wait(xp, p)
-        if p < 3:
-            partner_up[p].start()
-        if p > 0:
-            partner_down[p].start()
-    ag_wait(down + xl, 2, 3)
-    down_across.start()
-    ag_wait(up + xl, 1, 0)
-    up_across.start()
     remote(
-        w_in.at[w_rows_here], w_got, w_ss.at[6], w_rs.at[6], (across, xp)
+        w_in.at[w_rows_here], w_got, w_ss.at[9], w_rs.at[9], (across, xp)
     ).wait_recv()
     w_share.start()
     load_og.wait()
     load_w.wait()
+    ag_wait(down // 2, 2, 3)
+    ag_wait(up // 2, 1, 0)
     w_theirs = w_all.at[1 - xl, w_rows_mate]
-    remote(w_theirs, w_theirs, w_ss.at[7], w_rs.at[7], (mate, f)).wait_recv()
+    remote(w_theirs, w_theirs, w_ss.at[10], w_rs.at[10], (mate, f)).wait_recv()
     for c in range(2):
-        gbuf[2 * yy + c] = dot(og_all[f], w_all[c]).astype(BF16)
+        gbuf[2 * yy + c] = dot(og_all[yy], w_all[c]).astype(BF16)
     g_make(0, up)
     g_copy(0, up).start()
     g_make(1, down)
     g_copy(1, down).start()
-    for p in (0, 3, 1, 2):
-        ag_wait(far + xl, p)
-        far_across[p].start()
 
     def local_grads(h):
         q, k, v, g = q_of(h), k_of(h), v_of(h), g_of(h)
@@ -389,56 +370,49 @@
             for u in range(2):
                 local_grads(2 * column + u)
 
-    def at_copy(slot):
-        return remote(att_send.at[slot], att_all.at[f], at_ss.at[0], at_rs.at[0], (s, slot))
-
-    def at_all():
-        every = pl.ds(0, group - 1)
-        return remote(att_send.at[every], att_all.at[every], at_ss.at[0], at_rs.at[0], (mate, f))
+    def at_copy(row):
+        return remote(
+            att_send.at[row // 2], att_all.at[yy], at_ss.at[0], at_rs.at[0], (s, row + xl)
+        )
+
+    def at_every():
+        some = pl.ds(0, ring - 1)
+        return remote(att_send.at[some], att_all.at[some], at_ss.at[0], at_rs.at[0], (mate, f))
 
     qg[0].start()
     qg[0].spread()
+    ag_wait(far // 2, 0, 3, 1, 2)
+    g_make(2, far)
+    g_copy(2, far).start()
     kv.finish()
     kv.wait()
-    @pl.loop(0, HEADS // 2)
+    @pl.loop(0, ring)
     def _(i):
-        for u in range(2):
-            h = 2 * i + u
+        for u in range(HEADS // ring):
+            h = i * (HEADS // ring) + u
             attended = dot(q_of(h), state[0, h]) + acc_a[:, head_cols(h)]
             att_send[i, :, u * HEAD_DIM:(u + 1) * HEAD_DIM] = (factor * attended).astype(BF16)
 
-    att_all[f] = att_send[f]
-
-    @pl.loop(1, group)
-    def _(j):
-        at_copy((f + j) % group).start()
-
-    g_make(2, far)
-    g_copy(2, far).start()
+    att_all[yy] = att_send[yy]
+    for row in (up, down, far):
+        at_copy(row).start()
     local_pair(0)
     g_wait(up)
     qg[1].start()
     qg[1].spread()
-    local_pair(1)
     g_wait(down)
     qg[2].start()
     qg[2].spread()
-    local_pair(2)
+    local_pair(1)
+    qg[0].run()
     g_wait(far)
     qg[3].start()
     qg[3].spread()
-    qg[0].run()
-    local_pair(3)
-    for row in (down, up, far):
-        ag_wait(row + ol, 0, 1, 2, 3)
-
-    at_all().wait_recv()
 
     depth, width = w_in.shape
     out_rows = wg_ref.shape[0]
     step = 256
-    rows_all = group * BLOCK
-
+    rows_all = ring * BLOCK
     pairs_of_levels = levels // 2
 
     def w_part(p):
@@ -446,51 +420,65 @@
         def _(m):
             cols = pl.ds(pl.multiple_of((2 * m + p) * step, step), step)
             left = og_all[:, :, cols].reshape(rows_all, step)
-            piece = dot(left, att_all[...].reshape(rows_all, width), TN)
+            piece = dot(left, att_all[...].reshape(rows_all, 2 * width), TN)
             for n in range(2):
                 for c in range(2):
                     base = (2 * n + c) * out_rows
-                    part[c, n, p, m] = piece[base:base + out_rows]
+                    for x in range(2):
+                        rows = piece[base:base + out_rows, x * width:(x + 1) * width]
+                        part[c, n, x, p, m] = rows
 
     def w_pair(p):
         return remote(wp_send.at[p], wp_recv.at[p], w_ss.at[p], w_rs.at[p], (mate, f))
 
-    def w_cross(p):
-        return remote(wx_send.at[p], wx_recv.at[p], w_ss.at[2 + p], w_rs.at[2 + p], (across, f))
+    ring_x = ((xh, ol), (1 - xh, xl), (1 - xh, ol))
+
+    def w_cross(p, n):
+        xh_there, xl_there = ring_x[n]
+        to = ((2 * z + xh_there) * 2 + core, 2 * yy + xl_there)
+        at = 2 + 3 * p + n
+        return remote(wx_send.at[p, n], wx_recv.at[p, n], w_ss.at[at], w_rs.at[at], to)
 
     def w_level(p, m):
         to = (2 * (2 * m + p) + xh) * 2 + core
-        return remote(wz_send.at[p, m], wz_recv.at[z], w_ss.at[4], w_rs.at[4], (to, f))
+        return remote(wz_send.at[p, m], wz_recv.at[z], w_ss.at[8], w_rs.at[8], (to, f))
 
     def w_levels():
         every = wz_recv.at[pl.ds(0, levels - 1)]
-        return remote(every, every, w_ss.at[4], w_rs.at[4], (mate, f))
+        return remote(every, every, w_ss.at[8], w_rs.at[8], (mate, f))
 
     def w_pair_start(p):
         @pl.loop(0, pairs_of_levels)
         def _(m):
             for n in range(2):
-                wp_send[p, n, m] = part[1 - core, n, p, m].astype(BF16)
+                for x in range(2):
+                    wp_send[p, n, x, m] = part[1 - core, n, x, p, m].astype(BF16)
 
         w_pair(p).start()
 
     def w_cross_start(p):
         w_pair(p).wait_recv()
+        for n in (1, 0, 2):
+            xh_there, xl_there = ring_x[n]
+
+            @pl.loop(0, pairs_of_levels)
+            def _(m):
+                total = part[core, xh_there, xl_there, p, m]
+                total = total + wp_recv[p, xh_there, xl_there, m].astype(F32)
+                wx_send[p, n, m] = total.astype(BF16)
+
+            w_cross(p, n).start()
+
+    def w_level_start(p):
+        for n in range(3):
+            w_cross(p, n).wait_recv()
 
         @pl.loop(0, pairs_of_levels)
         def _(m):
-            total = part[core, 1 - xh, p, m] + wp_recv[p, 1 - xh, m].astype(F32)
-            wx_send[p, m] = total.astype(BF16)
-
-        w_cross(p).start()
-
-    def w_level_start(p):
-        w_cross(p).wait_recv()
-
-        @pl.loop(0, pairs_of_levels)
-        def _(m):
-            total = part[core, xh, p, m] + wp_recv[p, xh, m].astype(F32)
-            wz_send[p, m] = (total + wx_recv[p, m].astype(F32)).astype(BF16)
+            total = part[core, xh, xl, p, m] + wp_recv[p, xh, xl, m].astype(F32)
+            for n in range(3):
+                total = total + wx_recv[p, n, m].astype(F32)
+            wz_send[p, m] = total.astype(BF16)
 
         @pl.when(z % 2 == p)
         def _():
@@ -504,6 +492,7 @@
             def _():
                 w_level(p, m).start()
 
+    at_every().wait_recv()
     w_part(0)
     w_pair_start(0)
     w_part(1)
@@ -511,10 +500,11 @@
     qg[1].run()
     w_cross_start(0)
     qg[2].run()
+    w_cross_start(1)
     qg[3].run()
-    w_cross_start(1)
+    local_pair(2)
+    local_pair(3)
     qg[0].finish()
-    w_level_start(0)
 
     def final_pair(n):
         for column in pairs[n]:
@@ -531,25 +521,26 @@
     for n in range(3):
         qg[n].wait()
         final_pair(n)
+    w_level_start(0)
+    qg[3].finish()
     w_level_start(1)
-    qg[3].finish()
     qg[3].wait()
     final_pair(3)
-    passed = [*own, *own_across, *past_up, *past_down, *partner_up.values(), *partner_down.values()]
-    for copy in (*passed, *far_across.values(), down_across, up_across):
+    for copy in (*own, *past_up, *past_down):
         copy.wait_send()
 
     for n, row in enumerate((up, down, far)):
         g_copy(n, row).wait_send()
     w_side.wait_send()
     w_share.wait_send()
-    at_all().wait_send()
+    at_every().wait_send()
     kv.drain()
     for scan in qg:
         scan.drain()
     for p in range(2):
         w_pair(p).wait_send()
-        w_cross(p).wait_send()
+        for n in range(3):
+            w_cross(p, n).wait_send()
     w_levels().wait_recv()
     total = wz_recv[0].astype(F32)
     for j in range(1, levels):
@@ -580,6 +571,7 @@
     flat = (tokens, width_all)
     vmem = pl.BlockSpec(memory_space=pltpu.VMEM)
     levels = chips // 2
+    ring = group // 2
     pieces = (levels // 2, out_rows, width)
     blocks = pltpu.VMEM((group, tokens, width), BF16)
     square = (HEAD_DIM, HEAD_DIM)
@@ -603,11 +595,11 @@
             pltpu.VMEM(flat, BF16),
             pltpu.VMEM(flat, BF16),
             pltpu.VMEM((2, depth, width), BF16),
-            pltpu.VMEM((group, tokens, depth), BF16),
+            pltpu.VMEM((ring, tokens, depth), BF16),
             blocks,
             pltpu.VMEM((3, 2, tokens, width), BF16),
-            blocks,
-            blocks,
+            pltpu.VMEM((ring, tokens, 2 * width), BF16),
+            pltpu.VMEM((ring, tokens, 2 * width), BF16),
             pltpu.VMEM((half,) + square, F32),
             pltpu.VMEM((half,) + square, F32),
             pltpu.VMEM((half,) + square, F32),
@@ -622,26 +614,26 @@
             pltpu.VMEM(flat, F32),
             pltpu.VMEM(flat, F32),
             pltpu.VMEM(flat, F32),
-            pltpu.VMEM((2, 2, 2, levels // 2, out_rows, width), F32),
-            pltpu.VMEM((2, 2) + pieces, BF16),
-            pltpu.VMEM((2, 2) + pieces, BF16),
-            pltpu.VMEM((2,) + pieces, BF16),
-            pltpu.VMEM((2,) + pieces, BF16),
+            pltpu.VMEM((2, 2, 2, 2, levels // 2, out_rows, width), F32),
+            pltpu.VMEM((2, 2, 2) + pieces, BF16),
+            pltpu.VMEM((2, 2, 2) + pieces, BF16),
+            pltpu.VMEM((2, 3) + pieces, BF16),
+            pltpu.VMEM((2, 3) + pieces, BF16),
             pltpu.VMEM((2,) + pieces, BF16),
             pltpu.VMEM((levels, out_rows, width), BF16),
             dma((5,)),
-            dma((8, 4)),
-            dma((group, 4)),
+            dma((3, 4)),
+            dma((ring, 4)),
             dma((3,)),
-            dma((group // 2,)),
+            dma((ring,)),
             dma((1,)),
             dma((1,)),
             dma((10,)),
             dma((10,)),
             dma((10,)),
             dma((10,)),
-            dma((8,)),
-            dma((8,)),
+            dma((11,)),
+            dma((11,)),
         ],
         compiler_params=pltpu.CompilerParams(
             collective_id=0, has_side_effects=True, vmem_limit_bytes=44 * 1024 * 1024

time: 77.3 us -> 71.3 us (0.922)
  the two profiles are of different devices: /device:TPU:39 before, /device:TPU:1 now
where the time goes in v4:
time: 71.3 us; the launch traced here: 70 us
  Pallas kernels  69.4 us (97%)
    pallas_call x1, Pallas kernels, body(): pl.pallas_call(functools.partial(kernel, chips, group // 2, factor, grad_...  68.2 us

profile of v4, /device:TPU:1, one launch (start us, length us, event | category | flops | bytes accessed | tf_op | source)
XLA Modules:
  0.0 70.0 jit_solution(12258339531062696669)
XLA Ops:
  0.6 68.2 %shard_map.84 = (bf16[128,2048]{1,0:T(8,128)(2,1)S(1)}, bf16[128,2048]{1,0:T(8,128)(2,1)S(1)}, bf16[128,2048]{1,0:T(8,128)(2,1)S(1)}, f32[64,256]{1,0:T(8,128)S(1)}) custom-call(bf16[128,2048]{1,0:T(8,128)(2,1)} %bitcast.7, bf16[128,2048]{1,0:T(8,128)(2,1)} %bitcast.8, bf16[128,2048]{1,0:T(8,128)(2,1)} %bitcast.9, bf16[128,2048]{1,0:T(8,128)(2,1)} %bitcast.10, ...), custom_call_target="tpu_custom_call" | custom-call | tf_op jit(solution)/shard_map/pallas_call | solution.py:588
  68.9 1.2 %shard_map.85 = (bf16[128,2048]{1,0:T(8,128)(2,1)}, bf16[128,2048]{1,0:T(8,128)(2,1)}, bf16[128,2048]{1,0:T(8,128)(2,1)}, f32[64,256]{1,0:T(8,128)}) custom-call(bf16[128,2048]{1,0:T(8,128)(2,1)S(1)} %get-tuple-element.12.refs_0_, bf16[128,2048]{1,0:T(8,128)(2,1)S(1)} %get-tuple-element.13.refs_1_, bf16[128,2048]{1,0:T(8,128)(2,1)S(1)} %get-tuple-element.14.refs_2_, ...), custom_call_target="tpu_custom_call" | custom-call | tf_op jit(solution)/shard_map/pallas_call | solution.py:642

commit v5 on v4

--- a/solution.py
+++ b/solution.py
@@ -11,6 +11,7 @@
 HEADS = 16
 HEAD_DIM = 128
 BLOCK = 128
+PARTS = 4
 MESH = pl.DeviceIdType.MESH
 F32 = jnp.float32
 BF16 = jnp.bfloat16
@@ -159,10 +160,10 @@
     w_rows_here = pl.ds(core * w_part, w_part)
     w_rows_mate = pl.ds((1 - core) * w_part, w_part)
     w_side = remote(
-        w_in.at[w_rows_here], w_all.at[xl, w_rows_here], w_ss.at[9], w_rs.at[9], (across, xp)
+        w_in.at[w_rows_here], w_all.at[xl, w_rows_here], w_ss.at[4 * PARTS + 1], w_rs.at[4 * PARTS + 1], (across, xp)
     )
     w_got = w_all.at[1 - xl, w_rows_here]
-    w_share = remote(w_got, w_got, w_ss.at[10], w_rs.at[10], (mate, f))
+    w_share = remote(w_got, w_got, w_ss.at[4 * PARTS + 2], w_rs.at[4 * PARTS + 2], (mate, f))
 
     w_side.start()
     for p in range(4):
@@ -339,7 +340,7 @@
         past_down[n].start()
     kv.run()
     remote(
-        w_in.at[w_rows_here], w_got, w_ss.at[9], w_rs.at[9], (across, xp)
+        w_in.at[w_rows_here], w_got, w_ss.at[4 * PARTS + 1], w_rs.at[4 * PARTS + 1], (across, xp)
     ).wait_recv()
     w_share.start()
     load_og.wait()
@@ -347,7 +348,7 @@
     ag_wait(down // 2, 2, 3)
     ag_wait(up // 2, 1, 0)
     w_theirs = w_all.at[1 - xl, w_rows_mate]
-    remote(w_theirs, w_theirs, w_ss.at[10], w_rs.at[10], (mate, f)).wait_recv()
+    remote(w_theirs, w_theirs, w_ss.at[4 * PARTS + 2], w_rs.at[4 * PARTS + 2], (mate, f)).wait_recv()
     for c in range(2):
         gbuf[2 * yy + c] = dot(og_all[yy], w_all[c]).astype(BF16)
     g_make(0, up)
@@ -413,12 +414,12 @@
     out_rows = wg_ref.shape[0]
     step = 256
     rows_all = ring * BLOCK
-    pairs_of_levels = levels // 2
+    levels_of_part = levels // PARTS
 
     def w_part(p):
-        @pl.loop(0, pairs_of_levels)
+        @pl.loop(0, levels_of_part)
         def _(m):
-            cols = pl.ds(pl.multiple_of((2 * m + p) * step, step), step)
+            cols = pl.ds(pl.multiple_of((PARTS * m + p) * step, step), step)
             left = og_all[:, :, cols].reshape(rows_all, step)
             piece = dot(left, att_all[...].reshape(rows_all, 2 * width), TN)
             for n in range(2):
@@ -436,19 +437,19 @@
     def w_cross(p, n):
         xh_there, xl_there = ring_x[n]
         to = ((2 * z + xh_there) * 2 + core, 2 * yy + xl_there)
-        at = 2 + 3 * p + n
+        at = PARTS + 3 * p + n
         return remote(wx_send.at[p, n], wx_recv.at[p, n], w_ss.at[at], w_rs.at[at], to)
 
     def w_level(p, m):
-        to = (2 * (2 * m + p) + xh) * 2 + core
-        return remote(wz_send.at[p, m], wz_recv.at[z], w_ss.at[8], w_rs.at[8], (to, f))
+        to = (2 * (PARTS * m + p) + xh) * 2 + core
+        return remote(wz_send.at[p, m], wz_recv.at[z], w_ss.at[4 * PARTS], w_rs.at[4 * PARTS], (to, f))
 
     def w_levels():
         every = wz_recv.at[pl.ds(0, levels - 1)]
-        return remote(every, every, w_ss.at[8], w_rs.at[8], (mate, f))
+        return remote(every, every, w_ss.at[4 * PARTS], w_rs.at[4 * PARTS], (mate, f))
 
     def w_pair_start(p):
-        @pl.loop(0, pairs_of_levels)
+        @pl.loop(0, levels_of_part)
         def _(m):
             for n in range(2):
                 for x in range(2):
@@ -461,7 +462,7 @@
         for n in (1, 0, 2):
             xh_there, xl_there = ring_x[n]
 
-            @pl.loop(0, pairs_of_levels)
+            @pl.loop(0, levels_of_part)
             def _(m):
                 total = part[core, xh_there, xl_there, p, m]
                 total = total + wp_recv[p, xh_there, xl_there, m].astype(F32)
@@ -473,38 +474,41 @@
         for n in range(3):
             w_cross(p, n).wait_recv()
 
-        @pl.loop(0, pairs_of_levels)
+        @pl.loop(0, levels_of_part)
         def _(m):
             total = part[core, xh, xl, p, m] + wp_recv[p, xh, xl, m].astype(F32)
             for n in range(3):
                 total = total + wx_recv[p, n, m].astype(F32)
             wz_send[p, m] = total.astype(BF16)
 
-        @pl.when(z % 2 == p)
+        @pl.when(z % PARTS == p)
         def _():
-            wz_recv[z] = wz_send[p, z // 2]
-
-        @pl.loop(0, pairs_of_levels)
+            wz_recv[z] = wz_send[p, z // PARTS]
+
+        @pl.loop(0, levels_of_part)
         def _(j):
-            m = (z // 2 + j) % pairs_of_levels
-
-            @pl.when(2 * m + p != z)
+            m = (z // PARTS + j) % levels_of_part
+
+            @pl.when(PARTS * m + p != z)
             def _():
                 w_level(p, m).start()
 
     at_every().wait_recv()
     w_part(0)
     w_pair_start(0)
-    w_part(1)
-    w_pair_start(1)
+    for p in range(1, PARTS):
+        w_part(p)
+        w_pair_start(p)
+        w_cross_start(p - 1)
     qg[1].run()
-    w_cross_start(0)
     qg[2].run()
-    w_cross_start(1)
+    w_cross_start(PARTS - 1)
     qg[3].run()
     local_pair(2)
     local_pair(3)
     qg[0].finish()
+    w_level_start(0)
+    w_level_start(1)
 
     def final_pair(n):
         for column in pairs[n]:
@@ -521,9 +525,9 @@
     for n in range(3):
         qg[n].wait()
         final_pair(n)
-    w_level_start(0)
+    w_level_start(2)
     qg[3].finish()
-    w_level_start(1)
+    w_level_start(3)
     qg[3].wait()
     final_pair(3)
     for copy in (*own, *past_up, *past_down):
@@ -537,7 +541,7 @@
     kv.drain()
     for scan in qg:
         scan.drain()
-    for p in range(2):
+    for p in range(PARTS):
         w_pair(p).wait_send()
         for n in range(3):
             w_cross(p, n).wait_send()
@@ -572,7 +576,7 @@
     vmem = pl.BlockSpec(memory_space=pltpu.VMEM)
     levels = chips // 2
     ring = group // 2
-    pieces = (levels // 2, out_rows, width)
+    pieces = (levels // PARTS, out_rows, width)
     blocks = pltpu.VMEM((group, tokens, width), BF16)
     square = (HEAD_DIM, HEAD_DIM)
     chunk = (4, 2)
@@ -614,12 +618,12 @@
             pltpu.VMEM(flat, F32),
             pltpu.VMEM(flat, F32),
             pltpu.VMEM(flat, F32),
-            pltpu.VMEM((2, 2, 2, 2, levels // 2, out_rows, width), F32),
-            pltpu.VMEM((2, 2, 2) + pieces, BF16),
-            pltpu.VMEM((2, 2, 2) + pieces, BF16),
-            pltpu.VMEM((2, 3) + pieces, BF16),
-            pltpu.VMEM((2, 3) + pieces, BF16),
-            pltpu.VMEM((2,) + pieces, BF16),
+            pltpu.VMEM((2, 2, 2, PARTS, levels // PARTS, out_rows, width), F32),
+            pltpu.VMEM((PARTS, 2, 2) + pieces, BF16),
+            pltpu.VMEM((PARTS, 2, 2) + pieces, BF16),
+            pltpu.VMEM((PARTS, 3) + pieces, BF16),
+            pltpu.VMEM((PARTS, 3) + pieces, BF16),
+            pltpu.VMEM((PARTS,) + pieces, BF16),
             pltpu.VMEM((levels, out_rows, width), BF16),
             dma((5,)),
             dma((3, 4)),
@@ -632,8 +636,8 @@
             dma((10,)),
             dma((10,)),
             dma((10,)),
-            dma((11,)),
-            dma((11,)),
+            dma((4 * PARTS + 3,)),
+            dma((4 * PARTS + 3,)),
         ],
         compiler_params=pltpu.CompilerParams(
             collective_id=0, has_side_effects=True, vmem_limit_bytes=44 * 1024 * 1024

time: 71.3 us -> 69.1 us (0.969); the launches traced: 70 us -> 69 us
  Pallas kernels: 69.4 us -> 68.4 us
    pallas_call x1, Pallas kernels: 68.2 us -> 67.2 us  [body(): pl.pallas_call(functools.partial(kernel, chips, group // 2, factor, grad_...]
where the time goes in v5:
time: 69.1 us; the launch traced here: 69 us
  Pallas kernels  68.4 us (99%)
    pallas_call x1, Pallas kernels, body(): pl.pallas_call(functools.partial(kernel, chips, group // 2, factor, grad_...  67.2 us

profile of v5, /device:TPU:1, one launch (start us, length us, event | category | flops | bytes accessed | tf_op | source)
XLA Modules:
  0.0 69.0 jit_solution(9047389150508018053)
XLA Ops:
  0.6 67.2 %shard_map.84 = (bf16[128,2048]{1,0:T(8,128)(2,1)S(1)}, bf16[128,2048]{1,0:T(8,128)(2,1)S(1)}, bf16[128,2048]{1,0:T(8,128)(2,1)S(1)}, f32[64,256]{1,0:T(8,128)S(1)}) custom-call(bf16[128,2048]{1,0:T(8,128)(2,1)} %bitcast.7, bf16[128,2048]{1,0:T(8,128)(2,1)} %bitcast.8, bf16[128,2048]{1,0:T(8,128)(2,1)} %bitcast.9, bf16[128,2048]{1,0:T(8,128)(2,1)} %bitcast.10, ...), custom_call_target="tpu_custom_call" | custom-call | tf_op jit(solution)/shard_map/pallas_call | solution.py:592
  67.8 1.2 %shard_map.85 = (bf16[128,2048]{1,0:T(8,128)(2,1)}, bf16[128,2048]{1,0:T(8,128)(2,1)}, bf16[128,2048]{1,0:T(8,128)(2,1)}, f32[64,256]{1,0:T(8,128)}) custom-call(bf16[128,2048]{1,0:T(8,128)(2,1)S(1)} %get-tuple-element.12.refs_0_, bf16[128,2048]{1,0:T(8,128)(2,1)S(1)} %get-tuple-element.13.refs_1_, bf16[128,2048]{1,0:T(8,128)(2,1)S(1)} %get-tuple-element.14.refs_2_, ...), custom_call_target="tpu_custom_call" | custom-call | tf_op jit(solution)/shard_map/pallas_call | solution.py:646

commit v6 on v5

--- a/solution.py
+++ b/solution.py
@@ -509,6 +509,7 @@
     qg[0].finish()
     w_level_start(0)
     w_level_start(1)
+    w_level_start(2)
 
     def final_pair(n):
         for column in pairs[n]:
@@ -522,12 +523,11 @@
 
     for n in range(1, 3):
         qg[n].finish()
+    w_level_start(3)
     for n in range(3):
         qg[n].wait()
         final_pair(n)
-    w_level_start(2)
     qg[3].finish()
-    w_level_start(3)
     qg[3].wait()
     final_pair(3)
     for copy in (*own, *past_up, *past_down):

time: 69.1 us -> 68.2 us (0.987)
  Pallas kernels: 68.4 us -> 67.5 us
    pallas_call x1, Pallas kernels: 67.2 us -> 66.3 us  [body(): pl.pallas_call(functools.partial(kernel, chips, group // 2, factor, grad_...]
where the time goes in v6:
time: 68.2 us; the launch traced here: 68.1 us
  Pallas kernels  67.5 us (99%)
    pallas_call x1, Pallas kernels, body(): pl.pallas_call(functools.partial(kernel, chips, group // 2, factor, grad_...  66.3 us

profile of v6, /device:TPU:1, one launch (start us, length us, event | category | flops | bytes accessed | tf_op | source)
XLA Modules:
  0.0 68.1 jit_solution(2172069300229731127)
XLA Ops:
  0.6 66.3 %shard_map.84 = (bf16[128,2048]{1,0:T(8,128)(2,1)S(1)}, bf16[128,2048]{1,0:T(8,128)(2,1)S(1)}, bf16[128,2048]{1,0:T(8,128)(2,1)S(1)}, f32[64,256]{1,0:T(8,128)S(1)}) custom-call(bf16[128,2048]{1,0:T(8,128)(2,1)} %bitcast.7, bf16[128,2048]{1,0:T(8,128)(2,1)} %bitcast.8, bf16[128,2048]{1,0:T(8,128)(2,1)} %bitcast.9, bf16[128,2048]{1,0:T(8,128)(2,1)} %bitcast.10, ...), custom_call_target="tpu_custom_call" | custom-call | tf_op jit(solution)/shard_map/pallas_call | solution.py:592
  66.9 1.2 %shard_map.85 = (bf16[128,2048]{1,0:T(8,128)(2,1)}, bf16[128,2048]{1,0:T(8,128)(2,1)}, bf16[128,2048]{1,0:T(8,128)(2,1)}, f32[64,256]{1,0:T(8,128)}) custom-call(bf16[128,2048]{1,0:T(8,128)(2,1)S(1)} %get-tuple-element.12.refs_0_, bf16[128,2048]{1,0:T(8,128)(2,1)S(1)} %get-tuple-element.13.refs_1_, bf16[128,2048]{1,0:T(8,128)(2,1)S(1)} %get-tuple-element.14.refs_2_, ...), custom_call_target="tpu_custom_call" | custom-call | tf_op jit(solution)/shard_map/pallas_call | solution.py:646

commit v7 on v6

--- a/solution.py
+++ b/solution.py
@@ -397,14 +397,12 @@
     att_all[yy] = att_send[yy]
     for row in (up, down, far):
         at_copy(row).start()
-    local_pair(0)
     g_wait(up)
     qg[1].start()
     qg[1].spread()
     g_wait(down)
     qg[2].start()
     qg[2].spread()
-    local_pair(1)
     qg[0].run()
     g_wait(far)
     qg[3].start()
@@ -504,8 +502,8 @@
     qg[2].run()
     w_cross_start(PARTS - 1)
     qg[3].run()
-    local_pair(2)
-    local_pair(3)
+    for n in range(4):
+        local_pair(n)
     qg[0].finish()
     w_level_start(0)
     w_level_start(1)

time: 68.2 us -> 68.2 us (level)
  no operation moved by 1% of the time
where the time goes in v7:
time: 68.2 us; the launch traced here: 68.1 us
  Pallas kernels  67.5 us (99%)
    pallas_call x1, Pallas kernels, body(): pl.pallas_call(functools.partial(kernel, chips, group // 2, factor, grad_...  66.3 us

profile of v7, /device:TPU:1, one launch (start us, length us, event | category | flops | bytes accessed | tf_op | source)
XLA Modules:
  0.0 68.1 jit_solution(10852039894530353927)
XLA Ops:
  0.6 66.3 %shard_map.84 = (bf16[128,2048]{1,0:T(8,128)(2,1)S(1)}, bf16[128,2048]{1,0:T(8,128)(2,1)S(1)}, bf16[128,2048]{1,0:T(8,128)(2,1)S(1)}, f32[64,256]{1,0:T(8,128)S(1)}) custom-call(bf16[128,2048]{1,0:T(8,128)(2,1)} %bitcast.7, bf16[128,2048]{1,0:T(8,128)(2,1)} %bitcast.8, bf16[128,2048]{1,0:T(8,128)(2,1)} %bitcast.9, bf16[128,2048]{1,0:T(8,128)(2,1)} %bitcast.10, ...), custom_call_target="tpu_custom_call" | custom-call | tf_op jit(solution)/shard_map/pallas_call | solution.py:590
  66.9 1.2 %shard_map.85 = (bf16[128,2048]{1,0:T(8,128)(2,1)}, bf16[128,2048]{1,0:T(8,128)(2,1)}, bf16[128,2048]{1,0:T(8,128)(2,1)}, f32[64,256]{1,0:T(8,128)}) custom-call(bf16[128,2048]{1,0:T(8,128)(2,1)S(1)} %get-tuple-element.12.refs_0_, bf16[128,2048]{1,0:T(8,128)(2,1)S(1)} %get-tuple-element.13.refs_1_, bf16[128,2048]{1,0:T(8,128)(2,1)S(1)} %get-tuple-element.14.refs_2_, ...), custom_call_target="tpu_custom_call" | custom-call | tf_op jit(solution)/shard_map/pallas_call | solution.py:644
